TPU v7x, 256 devices: a whole 4x4x8 slice. The times are simulated.
256 devices in a mesh: gx: 32 (over x, y, core), gy: 8 (over z).
Axes of the slice: x: 4, y: 4, z: 8, core: 2. Of those that a mesh axis runs over, the one named last changes fastest.
Arguments:
- right_side: float32 [4096, 4096], P('gx', 'gy'), may hold values from -6 to 6
- kappa_field: float32 [4096, 4096], P('gx', 'gy'), may hold values from 0.0001 to 0.01
- ice_blocks: int32 [512, 512], P('gx', 'gy'), may hold values 0 or 1
Outputs:
- solution_field: float32 [4096, 4096], P('gx', 'gy')
All inputs are finite; a program needn't handle non-finite values. No bound on the sum of `ice_blocks` on one device may be relied on, other than what follows from the above.
Results may differ from a plain program's by a relative error of at most 0.0001.
Values sent between devices are 32-bit elements; how exact they have to be, the bound alone decides.
A program may use at most 64 MiB of HBM per device.

v0:
```python
import jax
import jax.numpy as jnp
from jax import lax
from jax.sharding import PartitionSpec as P

BLOCK = 8
NC = 16


damping = 0.8


def with_halo(cells, sides, width):
    for axis, dim in sides:
        count = lax.axis_size(axis)
        ends = count - 1
        head = lax.slice_in_dim(cells, 0, width, axis=dim)
        tail = lax.slice_in_dim(cells, cells.shape[dim] - width, cells.shape[dim], axis=dim)
        cells = jnp.concatenate(
            [
                lax.ppermute(tail, axis, [(i, (i + 1) % count) for i in range(ends)]),
                cells,
                lax.ppermute(head, axis, [((i + 1) % count, i) for i in range(ends)]),
            ],
            axis=dim,
        )
    return cells


def with_halo_2(x, sides, width):
    edges = {}
    for axis, dim in sides:
        devices, length = (lax.axis_size(axis), x.shape[dim])
        up = [(i, (i + 1) % devices) for i in range(devices - 1)]
        last = lax.slice_in_dim(x, length - width, length, axis=dim)
        first = lax.slice_in_dim(x, 0, width, axis=dim)
        edges[dim] = (
            lax.ppermute(last, axis, up),
            lax.ppermute(first, axis, [(b, a) for a, b in up]),
        )
    done = []
    for _, dim in sides:
        low, high = edges[dim]
        around = [(width, width) if d in done else (0, 0) for d in range(x.ndim)]
        x = jnp.concatenate([jnp.pad(low, around), x, jnp.pad(high, around)], axis=dim)
        done.append(dim)
    return x


def apply_operator(padded, reaction, stiffness):
    middle = padded[1:-1, 1:-1]
    beside = padded[2:, 1:-1] + padded[:-2, 1:-1]
    beside = beside + padded[1:-1, 2:] + padded[1:-1, :-2]
    return reaction * middle + stiffness * (4.0 * middle - beside)


def jacobi_step(padded, source, reaction, stiffness):
    middle = padded[1:-1, 1:-1]
    applied = apply_operator(padded, reaction, stiffness)
    return middle + damping * (source - applied) / (reaction + 4.0 * stiffness)


def restrict(field):
    height, width = field.shape
    return field.reshape(height // 2, 2, width // 2, 2).mean(axis=(1, 3))


def prolong(field):
    return jnp.repeat(jnp.repeat(field, 2, axis=0), 2, axis=1)


def extend(field, margin):
    return with_halo(field, (("gx", 0), ("gy", 1)), margin)


def level_margins(source, reaction):
    stacked = jnp.stack((source, reaction), axis=0)
    widened = with_halo_2(stacked, (("gx", 1), ("gy", 2)), 1)
    return (widened[0], widened[1])


def inside_region(height, width, margin):
    row_index = (
        lax.axis_index("gx") * height + jnp.arange(height + 2 * margin, dtype=jnp.int32) - margin
    )
    col_index = (
        lax.axis_index("gy") * width + jnp.arange(width + 2 * margin, dtype=jnp.int32) - margin
    )
    row_valid = (row_index >= 0) & (row_index < height * lax.axis_size("gx"))
    col_valid = (col_index >= 0) & (col_index < width * lax.axis_size("gy"))
    return (row_valid[:, None] & col_valid[None, :]).astype(jnp.float32)


def deep_sweeps(field, source, reaction, source_rim, reaction_rim, stiffness):
    height, width = field.shape
    keeper = inside_region(height, width, 1)
    wider = extend(field, 2)
    middle = jacobi_step(wider, source_rim, reaction_rim, stiffness) * keeper
    field = jacobi_step(middle, source, reaction, stiffness)
    return field


def smooth(field, source, reaction, stiffness, margins):
    field = deep_sweeps(field, source, reaction, margins[0], margins[1], stiffness)
    return field


def per_device(right_side, kappa_field, ice_blocks):
    ice = jnp.repeat(jnp.repeat(ice_blocks, BLOCK, axis=0), BLOCK, axis=1).astype(jnp.float32)
    reaction = kappa_field * (1.0 + 3.0 * (1.0 - ice))
    source = right_side
    stored = []
    for level in range(3):
        stiffness = 0.25**level
        margins = level_margins(source, reaction)
        field = smooth(jnp.zeros_like(source), source, reaction, stiffness, margins)
        stored.append((field, source, reaction, margins))
        residual = source - apply_operator(extend(field, 1), reaction, stiffness)
        source = restrict(residual)
        reaction = restrict(reaction)
    height, width = source.shape
    stacked = jnp.stack((source, reaction), axis=0)
    region = with_halo(stacked, (("gx", 1), ("gy", 2)), NC)
    region_source = region[0]
    region_reaction = region[1]
    keeper = inside_region(height, width, NC)
    coarse = jnp.zeros_like(region_source)
    for sweep in range(NC):
        coarse = jacobi_step(jnp.pad(coarse, 1), region_source, region_reaction, 0.25**3) * keeper
    field = coarse[NC : NC + height, NC : NC + width]
    for level in (2, 1, 0):
        stiffness = 0.25**level
        before, source, reaction, margins = stored[level]
        field = smooth(before + prolong(field), source, reaction, stiffness, margins)
    return field


def solution(mesh):
    in_specs = (P("gx", "gy"), P("gx", "gy"), P("gx", "gy"))
    out_specs = P("gx", "gy")
    return jax.shard_map(
        per_device, mesh=mesh, in_specs=in_specs, out_specs=out_specs, check_vma=False
    )
```

profile of v0, /device:TPU:38, one launch (start us, length us, event | category | flops | bytes accessed | tf_op | source)
XLA Modules:
  0.0 313.3 jit_solution(3471163264477591197)
XLA Ops:
  2.1 5.8 %collective-permute-start.1 = (f32[2,512]{0,1:T(8,128)S(1)}, f32[2,512]{0,1:T(8,128)S(1)}, u32[]{:S(2)}, u32[]{:S(2)}) collective-permute-start(f32[2,512]{0,1:T(8,128)S(1)} %broadcast.443), channel_id=1, source_target_pairs={{8,0},{16,8},{24,16},{32,24},{40,32},{48,40},{56,48},{64,56},{72,6... | collective-permute-start | bytes 12296 | tf_op jit(solution)/shard_map/ppermute | solution.py:23
  9.8 5.8 %collective-permute-start.21 = (f32[2,128]{1,0:T(2,128)S(1)}, f32[2,128]{1,0:T(2,128)S(1)}, u32[]{:S(2)}, u32[]{:S(2)}) collective-permute-start(f32[2,128]{1,0:T(2,128)S(1)} %broadcast.471), channel_id=1, source_target_pairs={{8,0},{16,8},{24,16},{32,24},{40,32},{48,40},{56,48},{64,56},{72,6... | collective-permute-start | bytes 3080 | tf_op jit(solution)/shard_map/ppermute | solution.py:23
  19.9 18.1 %reshape.171 = f32[64,2,256,2]{3,2,1,0:T(8,128)} reshape(f32[128,512]{1,0:T(8,128)S(1)} %copy.59) | data formatting | bytes 524288 | tf_op jit(solution)/shard_map/reshape | solution.py:65
  38.0 8.0 %reduce_sum.55 = f32[64,256]{1,0:T(8,128)S(1)} reduce(f32[64,2,256,2]{3,2,1,0:T(8,128)} %reshape.171, f32[]{:T(128)} %constant.49.clone.1), dimensions={1,3}, to_apply=%region_1.2 | reduce | flops 49152 | bytes 327684 | tf_op jit(solution)/shard_map/reduce_sum | solution.py:65
  46.1 5.8 %collective-permute-start.6 = (f32[2,1,512]{1,2,0:T(8,128)S(1)}, f32[2,1,512]{1,2,0:T(8,128)S(1)}, u32[]{:S(2)}, u32[]{:S(2)}) collective-permute-start(f32[2,1,512]{1,2,0:T(8,128)S(1)} %get-tuple-element.14), channel_id=1, source_target_pairs={{8,0},{16,8},{24,16},{32,24},{40,32},{48,40},{56,48},{64,56},{72,6... | collective-permute-start | bytes 12296 | tf_op jit(solution)/shard_map/ppermute | solution.py:39
  59.8 5.7 %collective-permute-start.9 = (f32[2,256]{1,0:T(2,128)S(1)}, f32[2,256]{1,0:T(2,128)S(1)}, u32[]{:S(2)}, u32[]{:S(2)}) collective-permute-start(f32[2,256]{1,0:T(2,128)S(1)} %broadcast.457), channel_id=1, source_target_pairs={{8,0},{16,8},{24,16},{32,24},{40,32},{48,40},{56,48},{64,56},{72,6... | collective-permute-start | bytes 6152 | tf_op jit(solution)/shard_map/ppermute | solution.py:23
  83.5 5.9 %collective-permute-done.13 = f32[1,512]{0,1:T(8,128)S(1)} collective-permute-done((f32[1,512]{0,1:T(8,128)S(1)}, f32[1,512]{0,1:T(8,128)S(1)}, u32[]{:S(2)}, u32[]{:S(2)}) %collective-permute-start.13) | collective-permute-done | bytes 2080 | tf_op jit(solution)/shard_map/ppermute | solution.py:21
  91.4 5.1 %collective-permute-start.15 = (f32[130,1]{0,1:T(1,128)S(1)}, f32[130,1]{0,1:T(1,128)S(1)}, u32[]{:S(2)}, u32[]{:S(2)}) collective-permute-start(f32[130,1]{0,1:T(1,128)S(1)} %get-tuple-element.10), channel_id=1, source_target_pairs={{0,1},{1,2},{2,3},{3,4},{4,5},{5,6},{6,7},{8,9},{9,10},{10,11},{11... | collective-permute-start | bytes 1568 | tf_op jit(solution)/shard_map/ppermute | solution.py:21
  96.6 5.1 %collective-permute-start.10 = (f32[68,2]{1,0:T(8,128)S(1)}, f32[68,2]{1,0:T(8,128)S(1)}, u32[]{:S(2)}, u32[]{:S(2)}) collective-permute-start(f32[68,2]{1,0:T(8,128)S(1)} %get-tuple-element.30), channel_id=1, source_target_pairs={{0,1},{1,2},{2,3},{3,4},{4,5},{5,6},{6,7},{8,9},{9,10},{10,11},{11... | collective-permute-start | bytes 1640 | tf_op jit(solution)/shard_map/ppermute | solution.py:21
  104.3 18.1 %reshape.170 = f32[64,2,256,2]{3,2,1,0:T(8,128)} reshape(f32[128,512]{1,0:T(8,128)S(1)} %copy.58) | data formatting | bytes 524288 | tf_op jit(solution)/shard_map/reshape | solution.py:65
  122.4 8.0 %reduce_sum.54 = f32[64,256]{1,0:T(8,128)S(1)} reduce(f32[64,2,256,2]{3,2,1,0:T(8,128)} %reshape.170, f32[]{:T(128)} %constant.49.clone.1), dimensions={1,3}, to_apply=%region_0.1 | reduce | flops 49152 | bytes 327684 | tf_op jit(solution)/shard_map/reduce_sum | solution.py:65
  132.4 5.8 %collective-permute-start.18 = (f32[2,1,256]{2,1,0:T(1,128)S(1)}, f32[2,1,256]{2,1,0:T(1,128)S(1)}, u32[]{:S(2)}, u32[]{:S(2)}) collective-permute-start(f32[2,1,256]{2,1,0:T(1,128)S(1)} %get-tuple-element.22), channel_id=1, source_target_pairs={{8,0},{16,8},{24,16},{32,24},{40,32},{48,40},{56,48},{64,56},{72,6... | collective-permute-start | bytes 6152 | tf_op jit(solution)/shard_map/ppermute | solution.py:39
  138.2 5.1 %collective-permute-start.16 = (f32[2,64,1]{2,1,0:T(8,128)S(1)}, f32[2,64,1]{2,1,0:T(8,128)S(1)}, u32[]{:S(2)}, u32[]{:S(2)}) collective-permute-start(f32[2,64,1]{2,1,0:T(8,128)S(1)} %get-tuple-element.23), channel_id=1, source_target_pairs={{0,1},{1,2},{2,3},{3,4},{4,5},{5,6},{6,7},{8,9},{9,10},{10,11},{11... | collective-permute-start | bytes 1544 | tf_op jit(solution)/shard_map/ppermute | solution.py:38
  171.3 5.6 %reshape.172 = f32[32,2,128,2]{3,2,1,0:T(8,128)} reshape(f32[64,256]{1,0:T(8,128)S(1)} %get-tuple-element.33) | data formatting | bytes 131072 | tf_op jit(solution)/shard_map/reshape | solution.py:65
  179.7 5.6 %div.128 = f32[32,2,128,2]{3,2,1,0:T(8,128)} reshape(f32[64,256]{1,0:T(8,128)S(1)} %get-tuple-element.34) | data formatting | bytes 131072 | tf_op jit(solution)/shard_map/div | solution.py:65
  190.1 5.8 %collective-permute-start.30 = (f32[2,1,128]{2,1,0:T(1,128)S(1)}, f32[2,1,128]{2,1,0:T(1,128)S(1)}, u32[]{:S(2)}, u32[]{:S(2)}) collective-permute-start(f32[2,1,128]{2,1,0:T(1,128)S(1)} %get-tuple-element.42), channel_id=1, source_target_pairs={{8,0},{16,8},{24,16},{32,24},{40,32},{48,40},{56,48},{64,56},{72,6... | collective-permute-start | bytes 3080 | tf_op jit(solution)/shard_map/ppermute | solution.py:39
  195.9 5.1 %collective-permute-start.28 = (f32[2,32,1]{2,1,0:T(8,128)S(1)}, f32[2,32,1]{2,1,0:T(8,128)S(1)}, u32[]{:S(2)}, u32[]{:S(2)}) collective-permute-start(f32[2,32,1]{2,1,0:T(8,128)S(1)} %get-tuple-element.43), channel_id=1, source_target_pairs={{0,1},{1,2},{2,3},{3,4},{4,5},{5,6},{6,7},{8,9},{9,10},{10,11},{11... | collective-permute-start | bytes 776 | tf_op jit(solution)/shard_map/ppermute | solution.py:38
  228.3 5.8 %collective-permute-start.37 = (f32[2,16,64]{2,1,0:T(8,128)S(1)}, f32[2,16,64]{2,1,0:T(8,128)S(1)}, u32[]{:S(2)}, u32[]{:S(2)}) collective-permute-start(f32[2,16,64]{2,1,0:T(8,128)S(1)} %pad_maximum_fusion.76), channel_id=1, source_target_pairs={{8,0},{16,8},{24,16},{32,24},{40,32},{48,40},{56,48},{64,56},{72,6... | collective-permute-start | bytes 24584 | tf_op jit(solution)/shard_map/ppermute | solution.py:23
  241.6 5.2 %collective-permute-done.39 = f32[2,48,16]{2,1,0:T(8,128)S(1)} collective-permute-done((f32[2,48,16]{2,1,0:T(8,128)S(1)}, f32[2,48,16]{2,1,0:T(8,128)S(1)}, u32[]{:S(2)}, u32[]{:S(2)}) %collective-permute-start.39) | collective-permute-done | bytes 6176 | tf_op jit(solution)/shard_map/ppermute | solution.py:23
  250.7 5.8 %collective-permute-start.41 = (f32[2,128]{1,0:T(2,128)S(1)}, f32[2,128]{1,0:T(2,128)S(1)}, u32[]{:S(2)}, u32[]{:S(2)}) collective-permute-start(f32[2,128]{1,0:T(2,128)S(1)} %get-tuple-element.52), channel_id=1, source_target_pairs={{8,0},{16,8},{24,16},{32,24},{40,32},{48,40},{56,48},{64,56},{72,6... | collective-permute-start | bytes 3080 | tf_op jit(solution)/shard_map/ppermute | solution.py:23
  257.9 5.4 %collective-permute-start.42 = (f32[36,2]{1,0:T(8,128)S(1)}, f32[36,2]{1,0:T(8,128)S(1)}, u32[]{:S(2)}, u32[]{:S(2)}) collective-permute-start(f32[36,2]{1,0:T(8,128)S(1)} %get-tuple-element.46), channel_id=1, source_target_pairs={{0,1},{1,2},{2,3},{3,4},{4,5},{5,6},{6,7},{8,9},{9,10},{10,11},{11... | collective-permute-start | bytes 872 | tf_op jit(solution)/shard_map/ppermute | solution.py:21
  265.2 4.9 %collective-permute-done.43 = f32[36,2]{1,0:T(8,128)S(1)} collective-permute-done((f32[36,2]{1,0:T(8,128)S(1)}, f32[36,2]{1,0:T(8,128)S(1)}, u32[]{:S(2)}, u32[]{:S(2)}) %collective-permute-start.43) | collective-permute-done | bytes 320 | tf_op jit(solution)/shard_map/ppermute | solution.py:23
  272.7 5.8 %collective-permute-start.45 = (f32[2,256]{1,0:T(2,128)S(1)}, f32[2,256]{1,0:T(2,128)S(1)}, u32[]{:S(2)}, u32[]{:S(2)}) collective-permute-start(f32[2,256]{1,0:T(2,128)S(1)} %get-tuple-element.32), channel_id=1, source_target_pairs={{8,0},{16,8},{24,16},{32,24},{40,32},{48,40},{56,48},{64,56},{72,6... | collective-permute-start | bytes 6152 | tf_op jit(solution)/shard_map/ppermute | solution.py:23
  292.6 5.8 %collective-permute-start.49 = (f32[2,512]{0,1:T(8,128)S(1)}, f32[2,512]{0,1:T(8,128)S(1)}, u32[]{:S(2)}, u32[]{:S(2)}) collective-permute-start(f32[2,512]{0,1:T(8,128)S(1)} %get-tuple-element.18), channel_id=1, source_target_pairs={{8,0},{16,8},{24,16},{32,24},{40,32},{48,40},{56,48},{64,56},{72,6... | collective-permute-start | bytes 12296 | tf_op jit(solution)/shard_map/ppermute | solution.py:23
  (212 shorter events, 149.1 us)
Async XLA Ops:
  0.0 55.7 %collective-permute-start = (f32[2,512]{0,1:T(8,128)S(1)}, f32[2,512]{0,1:T(8,128)S(1)}, u32[]{:S(2)}, u32[]{:S(2)}) collective-permute-start(f32[2,512]{0,1:T(8,128)S(1)} %broadcast.443), channel_id=1, source_target_pairs={{0,8},{8,16},{16,24},{24,32},{32,40},{40,48},{48,56},{56,64},{64,7... | collective-permute-start | bytes 12296 | tf_op jit(solution)/shard_map/ppermute | solution.py:21
  2.1 55.7 %collective-permute-start.1 = (f32[2,512]{0,1:T(8,128)S(1)}, f32[2,512]{0,1:T(8,128)S(1)}, u32[]{:S(2)}, u32[]{:S(2)}) collective-permute-start(f32[2,512]{0,1:T(8,128)S(1)} %broadcast.443), channel_id=1, source_target_pairs={{8,0},{16,8},{24,16},{32,24},{40,32},{48,40},{56,48},{64,56},{72,6... | collective-permute-start | bytes 12296 | tf_op jit(solution)/shard_map/ppermute | solution.py:23
  7.9 38.3 %collective-permute-start.20 = (f32[2,128]{1,0:T(2,128)S(1)}, f32[2,128]{1,0:T(2,128)S(1)}, u32[]{:S(2)}, u32[]{:S(2)}) collective-permute-start(f32[2,128]{1,0:T(2,128)S(1)} %broadcast.471), channel_id=1, source_target_pairs={{0,8},{8,16},{16,24},{24,32},{32,40},{40,48},{48,56},{56,64},{64,7... | collective-permute-start | bytes 3080 | tf_op jit(solution)/shard_map/ppermute | solution.py:21
  9.8 42.1 %collective-permute-start.21 = (f32[2,128]{1,0:T(2,128)S(1)}, f32[2,128]{1,0:T(2,128)S(1)}, u32[]{:S(2)}, u32[]{:S(2)}) collective-permute-start(f32[2,128]{1,0:T(2,128)S(1)} %broadcast.471), channel_id=1, source_target_pairs={{8,0},{16,8},{24,16},{32,24},{40,32},{48,40},{56,48},{64,56},{72,6... | collective-permute-start | bytes 3080 | tf_op jit(solution)/shard_map/ppermute | solution.py:23
  17.8 51.6 %collective-permute-start.5 = (f32[2,1,512]{1,2,0:T(8,128)S(1)}, f32[2,1,512]{1,2,0:T(8,128)}, u32[]{:S(2)}, u32[]{:S(2)}) collective-permute-start(f32[2,1,512]{1,2,0:T(8,128)S(1)} %get-tuple-element.13), channel_id=1, source_target_pairs={{0,8},{8,16},{16,24},{24,32},{32,40},{40,48},{48,56},{56,64},{64,7... | collective-permute-start | bytes 12296 | tf_op jit(solution)/shard_map/ppermute | solution.py:38
  46.1 25.3 %collective-permute-start.6 = (f32[2,1,512]{1,2,0:T(8,128)S(1)}, f32[2,1,512]{1,2,0:T(8,128)S(1)}, u32[]{:S(2)}, u32[]{:S(2)}) collective-permute-start(f32[2,1,512]{1,2,0:T(8,128)S(1)} %get-tuple-element.14), channel_id=1, source_target_pairs={{8,0},{16,8},{24,16},{32,24},{40,32},{48,40},{56,48},{64,56},{72,6... | collective-permute-start | bytes 12296 | tf_op jit(solution)/shard_map/ppermute | solution.py:39
  55.8 9.8 %collective-permute-start.7 = (f32[2,128,1]{1,2,0:T(1,128)S(1)}, f32[2,128,1]{1,2,0:T(1,128)S(1)}, u32[]{:S(2)}, u32[]{:S(2)}) collective-permute-start(f32[2,128,1]{1,2,0:T(1,128)S(1)} %get-tuple-element.16), channel_id=1, source_target_pairs={{1,0},{2,1},{3,2},{4,3},{5,4},{6,5},{7,6},{9,8},{10,9},{11,10},{12... | collective-permute-start | bytes 3080 | tf_op jit(solution)/shard_map/ppermute | solution.py:39
  57.8 24.2 %collective-permute-start.8 = (f32[2,256]{1,0:T(2,128)S(1)}, f32[2,256]{1,0:T(2,128)S(1)}, u32[]{:S(2)}, u32[]{:S(2)}) collective-permute-start(f32[2,256]{1,0:T(2,128)S(1)} %broadcast.457), channel_id=1, source_target_pairs={{0,8},{8,16},{16,24},{24,32},{32,40},{40,48},{48,56},{56,64},{64,7... | collective-permute-start | bytes 6152 | tf_op jit(solution)/shard_map/ppermute | solution.py:21
  59.8 22.2 %collective-permute-start.9 = (f32[2,256]{1,0:T(2,128)S(1)}, f32[2,256]{1,0:T(2,128)S(1)}, u32[]{:S(2)}, u32[]{:S(2)}) collective-permute-start(f32[2,256]{1,0:T(2,128)S(1)} %broadcast.457), channel_id=1, source_target_pairs={{8,0},{16,8},{24,16},{32,24},{40,32},{48,40},{56,48},{64,56},{72,6... | collective-permute-start | bytes 6152 | tf_op jit(solution)/shard_map/ppermute | solution.py:23
  79.6 9.8 %collective-permute-start.13 = (f32[1,512]{0,1:T(8,128)S(1)}, f32[1,512]{0,1:T(8,128)S(1)}, u32[]{:S(2)}, u32[]{:S(2)}) collective-permute-start(f32[1,512]{0,1:T(8,128)S(1)} %get-tuple-element.19), channel_id=1, source_target_pairs={{0,8},{8,16},{16,24},{24,32},{32,40},{40,48},{48,56},{56,64},{64,7... | collective-permute-start | bytes 6152 | tf_op jit(solution)/shard_map/ppermute | solution.py:21
  89.5 14.2 %collective-permute-start.14 = (f32[130,1]{0,1:T(1,128)S(1)}, f32[130,1]{0,1:T(1,128)S(1)}, u32[]{:S(2)}, u32[]{:S(2)}) collective-permute-start(f32[130,1]{0,1:T(1,128)S(1)} %get-tuple-element.9), channel_id=1, source_target_pairs={{1,0},{2,1},{3,2},{4,3},{5,4},{6,5},{7,6},{9,8},{10,9},{11,10},{12... | collective-permute-start | bytes 1568 | tf_op jit(solution)/shard_map/ppermute | solution.py:23
  91.4 12.3 %collective-permute-start.15 = (f32[130,1]{0,1:T(1,128)S(1)}, f32[130,1]{0,1:T(1,128)S(1)}, u32[]{:S(2)}, u32[]{:S(2)}) collective-permute-start(f32[130,1]{0,1:T(1,128)S(1)} %get-tuple-element.10), channel_id=1, source_target_pairs={{0,1},{1,2},{2,3},{3,4},{4,5},{5,6},{6,7},{8,9},{9,10},{10,11},{11... | collective-permute-start | bytes 1568 | tf_op jit(solution)/shard_map/ppermute | solution.py:21
  96.6 46.7 %collective-permute-start.10 = (f32[68,2]{1,0:T(8,128)S(1)}, f32[68,2]{1,0:T(8,128)S(1)}, u32[]{:S(2)}, u32[]{:S(2)}) collective-permute-start(f32[68,2]{1,0:T(8,128)S(1)} %get-tuple-element.30), channel_id=1, source_target_pairs={{0,1},{1,2},{2,3},{3,4},{4,5},{5,6},{6,7},{8,9},{9,10},{10,11},{11... | collective-permute-start | bytes 1640 | tf_op jit(solution)/shard_map/ppermute | solution.py:21
  101.8 43.7 %collective-permute-start.11 = (f32[68,2]{1,0:T(8,128)S(1)}, f32[68,2]{1,0:T(8,128)S(1)}, u32[]{:S(2)}, u32[]{:S(2)}) collective-permute-start(f32[68,2]{1,0:T(8,128)S(1)} %get-tuple-element.29), channel_id=1, source_target_pairs={{1,0},{2,1},{3,2},{4,3},{5,4},{6,5},{7,6},{9,8},{10,9},{11,10},{12... | collective-permute-start | bytes 1640 | tf_op jit(solution)/shard_map/ppermute | solution.py:23
  130.5 19.2 %collective-permute-start.17 = (f32[2,1,256]{2,1,0:T(1,128)S(1)}, f32[2,1,256]{2,1,0:T(1,128)S(1)}, u32[]{:S(2)}, u32[]{:S(2)}) collective-permute-start(f32[2,1,256]{2,1,0:T(1,128)S(1)} %get-tuple-element.21), channel_id=1, source_target_pairs={{0,8},{8,16},{16,24},{24,32},{32,40},{40,48},{48,56},{56,64},{64,7... | collective-permute-start | bytes 6152 | tf_op jit(solution)/shard_map/ppermute | solution.py:38
  132.4 17.3 %collective-permute-start.18 = (f32[2,1,256]{2,1,0:T(1,128)S(1)}, f32[2,1,256]{2,1,0:T(1,128)S(1)}, u32[]{:S(2)}, u32[]{:S(2)}) collective-permute-start(f32[2,1,256]{2,1,0:T(1,128)S(1)} %get-tuple-element.22), channel_id=1, source_target_pairs={{8,0},{16,8},{24,16},{32,24},{40,32},{48,40},{56,48},{64,56},{72,6... | collective-permute-start | bytes 6152 | tf_op jit(solution)/shard_map/ppermute | solution.py:39
  159.2 12.0 %collective-permute-start.26 = (f32[66,1]{1,0:T(8,128)S(1)}, f32[66,1]{1,0:T(8,128)S(1)}, u32[]{:S(2)}, u32[]{:S(2)}) collective-permute-start(f32[66,1]{1,0:T(8,128)S(1)} %get-tuple-element.27), channel_id=1, source_target_pairs={{1,0},{2,1},{3,2},{4,3},{5,4},{6,5},{7,6},{9,8},{10,9},{11,10},{12... | collective-permute-start | bytes 800 | tf_op jit(solution)/shard_map/ppermute | solution.py:23
  161.2 10.0 %collective-permute-start.27 = (f32[66,1]{1,0:T(8,128)S(1)}, f32[66,1]{1,0:T(8,128)S(1)}, u32[]{:S(2)}, u32[]{:S(2)}) collective-permute-start(f32[66,1]{1,0:T(8,128)S(1)} %get-tuple-element.28), channel_id=1, source_target_pairs={{0,1},{1,2},{2,3},{3,4},{4,5},{5,6},{6,7},{8,9},{9,10},{10,11},{11... | collective-permute-start | bytes 800 | tf_op jit(solution)/shard_map/ppermute | solution.py:21
  165.1 35.9 %collective-permute-start.22 = (f32[36,2]{1,0:T(8,128)S(1)}, f32[36,2]{1,0:T(8,128)S(1)}, u32[]{:S(2)}, u32[]{:S(2)}) collective-permute-start(f32[36,2]{1,0:T(8,128)S(1)} %get-tuple-element.50), channel_id=1, source_target_pairs={{0,1},{1,2},{2,3},{3,4},{4,5},{5,6},{6,7},{8,9},{9,10},{10,11},{11... | collective-permute-start | bytes 872 | tf_op jit(solution)/shard_map/ppermute | solution.py:21
  169.3 33.7 %collective-permute-start.23 = (f32[36,2]{1,0:T(8,128)S(1)}, f32[36,2]{1,0:T(8,128)S(1)}, u32[]{:S(2)}, u32[]{:S(2)}) collective-permute-start(f32[36,2]{1,0:T(8,128)S(1)} %get-tuple-element.49), channel_id=1, source_target_pairs={{1,0},{2,1},{3,2},{4,3},{5,4},{6,5},{7,6},{9,8},{10,9},{11,10},{12... | collective-permute-start | bytes 872 | tf_op jit(solution)/shard_map/ppermute | solution.py:23
  188.2 18.6 %collective-permute-start.29 = (f32[2,1,128]{2,1,0:T(1,128)S(1)}, f32[2,1,128]{2,1,0:T(1,128)S(1)}, u32[]{:S(2)}, u32[]{:S(2)}) collective-permute-start(f32[2,1,128]{2,1,0:T(1,128)S(1)} %get-tuple-element.41), channel_id=1, source_target_pairs={{0,8},{8,16},{16,24},{24,32},{32,40},{40,48},{48,56},{56,64},{64,7... | collective-permute-start | bytes 3080 | tf_op jit(solution)/shard_map/ppermute | solution.py:38
  190.1 16.7 %collective-permute-start.30 = (f32[2,1,128]{2,1,0:T(1,128)S(1)}, f32[2,1,128]{2,1,0:T(1,128)S(1)}, u32[]{:S(2)}, u32[]{:S(2)}) collective-permute-start(f32[2,1,128]{2,1,0:T(1,128)S(1)} %get-tuple-element.42), channel_id=1, source_target_pairs={{8,0},{16,8},{24,16},{32,24},{40,32},{48,40},{56,48},{64,56},{72,6... | collective-permute-start | bytes 3080 | tf_op jit(solution)/shard_map/ppermute | solution.py:39
  290.6 9.8 %collective-permute-start.48 = (f32[2,512]{0,1:T(8,128)S(1)}, f32[2,512]{0,1:T(8,128)S(1)}, u32[]{:S(2)}, u32[]{:S(2)}) collective-permute-start(f32[2,512]{0,1:T(8,128)S(1)} %get-tuple-element.17), channel_id=1, source_target_pairs={{0,8},{8,16},{16,24},{24,32},{32,40},{40,48},{48,56},{56,64},{64,7... | collective-permute-start | bytes 12296 | tf_op jit(solution)/shard_map/ppermute | solution.py:21
  292.6 9.6 %collective-permute-start.49 = (f32[2,512]{0,1:T(8,128)S(1)}, f32[2,512]{0,1:T(8,128)S(1)}, u32[]{:S(2)}, u32[]{:S(2)}) collective-permute-start(f32[2,512]{0,1:T(8,128)S(1)} %get-tuple-element.18), channel_id=1, source_target_pairs={{8,0},{16,8},{24,16},{32,24},{40,32},{48,40},{56,48},{64,56},{72,6... | collective-permute-start | bytes 12296 | tf_op jit(solution)/shard_map/ppermute | solution.py:23
  (29 other events, 201.0 us)
where the time goes:
time: 316 us; the launch traced here: 313 us
  starting transfers between devices  173 us (55%)
  waiting for transfers between devices  53.6 us (17%)
  local copies, waits for them, and re-layouts  53.3 us (17%)
  other arithmetic  32.5 us (10%)
    ppermute x20, starting transfers between devices, with_halo(): lax.ppermute(head, axis, [((i + 1) % count, i) for i in range(ends)])  66.1 us
    ppermute x20, starting transfers between devices, with_halo(): lax.ppermute(tail, axis, [(i, (i + 1) % count) for i in range(ends)])  63.4 us
    reshape x4, local copies, waits for them, and re-layouts, restrict(): return field.reshape(height // 2, 2, width // 2, 2).mean(axis=(1, 3))  42.8 us
    ppermute x20, waiting for transfers between devices, with_halo(): lax.ppermute(head, axis, [((i + 1) % count, i) for i in range(ends)])  26.8 us
    ppermute x6, starting transfers between devices, with_halo_2(): lax.ppermute(first, axis, [(b, a) for a, b in up])  23.3 us
    reduce_sum x6, other arithmetic, restrict(): return field.reshape(height // 2, 2, width // 2, 2).mean(axis=(1, 3))  22.1 us
    ppermute x6, starting transfers between devices, with_halo_2(): lax.ppermute(last, axis, up)  19.8 us
    ppermute x20, waiting for transfers between devices, with_halo(): lax.ppermute(tail, axis, [(i, (i + 1) % count) for i in range(ends)])  18.9 us
  transfers between devices with their start and end apart: 52, of which 17 were waited for; matrix products, arithmetic and copies ran while one was open for 24% of the time, Pallas kernels for 0%

commit v1 on v0

v1 whole, which is shorter than its diff:
```python
import functools

import jax
import jax.numpy as jnp
from jax import lax
from jax.experimental import pallas as pl
from jax.experimental.pallas import tpu as pltpu
from jax.sharding import PartitionSpec as P

MESH = pl.DeviceIdType.MESH
F32 = jnp.float32
BF16 = jnp.bfloat16
NC = 16
DAMP = 0.8


DIRS = ((-1, -1), (-1, 1), (1, -1), (1, 1), (0, -1), (0, 1), (-1, 0), (1, 0))


def lanes_of(shape):
    return lax.broadcasted_iota(jnp.int32, shape, len(shape) - 1)


def rows_of(shape):
    return lax.broadcasted_iota(jnp.int32, shape, len(shape) - 2)


def split(x):
    high = x.astype(BF16)
    low = (x - high.astype(F32)).astype(BF16)
    return high, low


def matmul(x, table):
    high, low = split(x)
    return jnp.dot(high, table, preferred_element_type=F32) + jnp.dot(low, table, preferred_element_type=F32)


def side_sum_0(x, lane):
    a = pltpu.roll(x, 1, 2)
    b = pltpu.roll(x, 127, 2)
    left = jnp.where(lane == 0, jnp.concatenate([a[4:5], a[0:4]], axis=0), a)
    right = jnp.where(lane == 127, jnp.concatenate([b[1:5], b[0:1]], axis=0), b)
    return left + right


def beside_planes(v, count):
    out = []
    for kr in range(count):
        row = []
        for kc in range(count):
            up = v[kr - 1][kc] if kr > 0 else pltpu.roll(v[count - 1][kc], 1, 0)
            down = v[kr + 1][kc] if kr < count - 1 else pltpu.roll(v[0][kc], 23, 0)
            left = v[kr][kc - 1] if kc > 0 else pltpu.roll(v[kr][count - 1], 1, 1)
            right = v[kr][kc + 1] if kc < count - 1 else pltpu.roll(v[kr][0], 127, 1)
            row.append((up + down) + (left + right))
        out.append(row)
    return out


def kernel(
    gx_size, gy_size,
    rs_hbm, kappa_hbm, ice_hbm, out_hbm,
    field, ice, w0, v1, v2, src0, lhs, down_table, up_table, snd, rcv, t3, rb, region, out_vmem,
    local_sem, out_sem, ssem1, rsem1, ssem2, rsem2,
):
    gx = lax.axis_index("gx")
    gy = lax.axis_index("gy")

    def there(dx, dy):
        return (gx + dx >= 0) & (gx + dx < gx_size) & (gy + dy >= 0) & (gy + dy < gy_size)

    barrier = pltpu.get_barrier_semaphore()
    count = jnp.int32(0)
    for dx, dy in DIRS:
        here = there(dx, dy)
        count = count + here.astype(jnp.int32)

        @pl.when(here)
        def _():
            pl.semaphore_signal(barrier, inc=1, device_id=(gx + dx, gy + dy), device_id_type=MESH)

    loads = [pltpu.make_async_copy(ice_hbm, ice, local_sem.at[8])]
    for c in range(4):
        for a, ref in ((1, kappa_hbm), (0, rs_hbm)):
            loads.append(
                pltpu.make_async_copy(
                    ref.at[:, pl.ds(c * 128, 128)], field.at[a, c, pl.ds(0, 128), :], local_sem.at[a * 4 + c]
                )
            )
    for load in loads:
        load.start()

    @pl.when(gx == 0)
    def _():
        field[:, 0:4, 160:192, :] = jnp.zeros((2, 4, 32, 128), F32)
        rcv[:, :, 40:48, :] = jnp.zeros((2, 2, 8, 128), F32)

    @pl.when(gx == gx_size - 1)
    def _():
        field[:, 0:4, 128:160, :] = jnp.zeros((2, 4, 32, 128), F32)
        rcv[:, :, 32:40, :] = jnp.zeros((2, 2, 8, 128), F32)

    @pl.when(gy == 0)
    def _():
        rcv[0] = jnp.zeros((2, 48, 128), F32)

    @pl.when(gy == gy_size - 1)
    def _():
        rcv[1] = jnp.zeros((2, 48, 128), F32)

    for i, (dx, dy) in enumerate(DIRS):
        @pl.when(jnp.logical_not(there(-dx, -dy)))
        def _():
            rb[i] = jnp.zeros((2, 24, 128), F32)

    fine = lax.broadcasted_iota(jnp.int32, (640, 512), 0)
    col = jnp.where(fine >= 608, fine - 640, fine)
    plane_lane = lax.broadcasted_iota(jnp.int32, (640, 512), 1)
    target = 8 * ((plane_lane & 127) - 32) + 2 * (plane_lane >> 7)
    near = ((col & -2) == target) & ((fine < 544) | (fine >= 608))
    down_table[...] = jnp.where(near, 0.25, 0.0).astype(BF16)
    fine = lax.broadcasted_iota(jnp.int32, (512, 640), 1)
    col = jnp.where(fine >= 608, fine - 640, fine)
    plane_lane = lax.broadcasted_iota(jnp.int32, (512, 640), 0)
    target = 8 * ((plane_lane & 127) - 32) + 2 * (plane_lane >> 7)
    near = ((col & -2) == target) & ((fine < 544) | (fine >= 608))
    up_table[...] = jnp.where(near, 1.0, 0.0).astype(BF16)

    loads[0].wait()
    spread = lax.broadcasted_iota(jnp.int32, (64, 512), 0) == (lax.broadcasted_iota(jnp.int32, (64, 512), 1) >> 3)
    wide = jnp.dot(
        ice[...].astype(F32).astype(BF16), jnp.where(spread, 1.0, 0.0).astype(BF16), preferred_element_type=F32
    )
    factor = 1.0 + 3.0 * (1.0 - wide)
    for load in loads[1:]:
        load.wait()
    for c in range(4):
        kappa = field[1, c, 0:128, :].reshape(16, 8, 128)
        own = kappa * factor[:, c * 128 : (c + 1) * 128].reshape(16, 1, 128)
        field[1, c, 0:128, :] = own.reshape(128, 128)

    lane8 = lanes_of((8, 128))
    for a in range(2):
        for tt in range(4):
            right = field[a, 3, 32 * tt : 32 * tt + 8, :]
            left = field[a, 0, 32 * tt : 32 * tt + 8, :]
            packed_right = pltpu.roll(right, 32, 1)
            packed_left = left
            for g in range(1, 4):
                start = 32 * tt + 8 * g
                right = field[a, 3, start : start + 8, :]
                left = field[a, 0, start : start + 8, :]
                inside = (lane8 >> 5) == g
                packed_right = jnp.where(inside, pltpu.roll(right, (32 + 32 * g) % 128, 1) if g < 3 else right, packed_right)
                packed_left = jnp.where(inside, pltpu.roll(left, 32 * g, 1), packed_left)
            snd[0, a, 8 * tt : 8 * tt + 8, :] = packed_right
            snd[1, a, 8 * tt : 8 * tt + 8, :] = packed_left

    pl.semaphore_wait(barrier, count)

    def first(i):
        dx, dy = DIRS[i]
        if dy == 0:
            src = field.at[:, pl.ds(0, 4), pl.ds(0 if dx < 0 else 96, 32), :]
            dst = field.at[:, pl.ds(0, 4), pl.ds(128 if dx < 0 else 160, 32), :]
        elif dx == 0:
            side = 0 if dy > 0 else 1
            src = snd.at[side]
            dst = rcv.at[side, :, pl.ds(0, 32), :]
        else:
            side = 0 if dy > 0 else 1
            src = snd.at[side, :, pl.ds(0 if dx < 0 else 24, 8), :]
            dst = rcv.at[side, :, pl.ds(32 if dx < 0 else 40, 8), :]
        return pltpu.make_async_remote_copy(
            src_ref=src, dst_ref=dst, send_sem=ssem1.at[i], recv_sem=rsem1.at[i],
            device_id=(gx + dx, gy + dy), device_id_type=MESH,
        )

    def second(i):
        dx, dy = DIRS[i]
        return pltpu.make_async_remote_copy(
            src_ref=t3, dst_ref=rb.at[i], send_sem=ssem2.at[i], recv_sem=rsem2.at[i],
            device_id=(gx + dx, gy + dy), device_id_type=MESH,
        )

    def on_all(make, action, sign):
        for i, (dx, dy) in enumerate(DIRS):
            @pl.when(there(sign * dx, sign * dy))
            def _():
                getattr(make(i), action)()

    on_all(first, "start", 1)
    on_all(first, "wait_recv", -1)

    even = ((lane8 >> 5) & 1) == 0
    used = (lane8 < 32) | (lane8 >= 96)
    for a in range(2):
        for tt in range(6):
            from_left = rcv[0, a, 8 * tt : 8 * tt + 8, :]
            from_right = pltpu.roll(rcv[1, a, 8 * tt : 8 * tt + 8, :], 32, 1)
            mixed = (jnp.where(even, from_left, from_right), jnp.where(even, from_right, from_left))
            for g in range(4):
                x = mixed[g % 2]
                x = pltpu.roll(x, 96 - 32 * g, 1) if g < 3 else x
                start = 32 * tt + 8 * g
                field[a, 4, start : start + 8, :] = jnp.where(used, x, 0.0)

    row = rows_of((24, 128))
    lane = lanes_of((24, 128))
    row_in = ((row < 16) | ((row < 20) & (gx < gx_size - 1))) | ((row >= 20) & (gx > 0))
    right_in = gy < gy_size - 1
    left_in = gy > 0
    tile_in = row_in & (((lane < 32) & right_in) | ((lane >= 96) & left_in))
    plane_in = row_in & (((lane >= 32) & (lane < 96)) | ((lane >= 96) & right_in) | ((lane < 32) & left_in))
    mask0 = jnp.stack([row_in.astype(F32)] * 4 + [tile_in.astype(F32)]) > 0.5
    lane5 = lanes_of((5, 24, 128))

    def planes0(ref, kr):
        return jnp.stack([ref[c, pl.ds(kr, 24, 8), :] for c in range(5)])

    def put(ref, kr, x):
        ref[kr + 1] = x
        if kr == 7:
            ref[0] = pltpu.roll(x, 1, 1)
        if kr == 0:
            ref[9] = pltpu.roll(x, 23, 1)

    def beside0(ref, kr):
        return (ref[kr] + ref[kr + 2]) + side_sum_0(ref[kr + 1], lane5)

    pair = None
    for kr in range(8):
        r = planes0(field.at[1], kr)
        b = planes0(field.at[0], kr)
        w = jnp.where(mask0, DAMP / (r + 4.0), 0.0)
        w0[kr] = w
        src0[kr] = b
        put(v1, kr, w * b)
        if kr % 2 == 0:
            pair = r
        else:
            r = r + pair
            for c in range(5):
                lhs[24 * (kr // 2) : 24 * (kr // 2) + 24, c * 128 : (c + 1) * 128] = r[c]
    reaction1 = matmul(lhs[...], down_table[...])
    for kr in range(8):
        put(v2, kr, 1.2 * v1[kr + 1] + w0[kr] * beside0(v1, kr))
    for kr in range(8):
        r = planes0(field.at[1], kr)
        rest = (src0[kr] - (r + 4.0) * v2[kr + 1]) + beside0(v2, kr)
        if kr % 2 == 0:
            pair = rest
        else:
            rest = rest + pair
            for c in range(5):
                lhs[24 * (kr // 2) : 24 * (kr // 2) + 24, c * 128 : (c + 1) * 128] = rest[c]
    source1 = matmul(lhs[...], down_table[...])

    def cut(x, n):
        return [[x[24 * i : 24 * i + 24, 128 * j : 128 * j + 128] for j in range(n)] for i in range(n)]

    def coarsen(x, n):
        return [
            [
                0.25 * ((x[2 * i][2 * j] + x[2 * i + 1][2 * j]) + (x[2 * i][2 * j + 1] + x[2 * i + 1][2 * j + 1]))
                for j in range(n)
            ]
            for i in range(n)
        ]

    def grid_of(n, make):
        return [[make(i, j) for j in range(n)] for i in range(n)]

    levels = []
    source, reaction = cut(source1, 4), cut(reaction1, 4)
    for level, n in ((1, 4), (2, 2)):
        s = 0.25**level
        d = grid_of(n, lambda i, j: reaction[i][j] + 4.0 * s)
        w = grid_of(n, lambda i, j: jnp.where(plane_in, DAMP / d[i][j], 0.0))
        wb = grid_of(n, lambda i, j: w[i][j] * source[i][j])
        near1 = beside_planes(wb, n)
        pre = grid_of(n, lambda i, j: 1.2 * wb[i][j] + (s * w[i][j]) * near1[i][j])
        near2 = beside_planes(pre, n)
        rest = grid_of(n, lambda i, j: (source[i][j] - d[i][j] * pre[i][j]) + s * near2[i][j])
        levels.append((n, s, w, wb, pre))
        source, reaction = coarsen(rest, n // 2), coarsen(reaction, n // 2)

    t3[0] = source[0][0]
    t3[1] = reaction[0][0]
    on_all(second, "start", 1)
    on_all(second, "wait_recv", -1)

    lane8 = lanes_of((8, 128))
    sub8 = rows_of((8, 128))
    own8 = (lane8 >= 32) & (lane8 < 96)
    high8 = lane8 >= 64

    def arrived(dx, dy):
        return rb.at[DIRS.index((-dx, -dy))]

    def joined(a, dx, start):
        middle = t3[a, start : start + 8, :] if dx == 0 else arrived(dx, 0)[a, start : start + 8, :]
        left = arrived(dx, -1)[a, start : start + 8, :]
        right = arrived(dx, 1)[a, start : start + 8, :]
        return jnp.where(own8, middle, pltpu.roll(jnp.where(high8, left, right), 64, 1))

    s3 = 0.25**3
    for t in range(7):
        if t == 4:
            parts = [jnp.where(sub8 == 7, joined(a, -1, 16), joined(a, 1, 16)) for a in range(2)]
        else:
            dx, start = ((0, 0), (0, 8), (1, 0), (1, 8), None, (-1, 0), (-1, 8))[t]
            parts = [joined(a, dx, start) for a in range(2)]
        spot = 8 * t + sub8
        spot = jnp.where(spot >= 36, spot - 56, spot) + 16 * gx
        side = lane8 - 32 + 64 * gy
        inside = (spot >= 0) & (spot < 16 * gx_size) & (side >= 0) & (side < 64 * gy_size)
        w = jnp.where(inside, DAMP / (parts[1] + 4.0 * s3), 0.0)
        region[0, 8 * t : 8 * t + 8, :] = w * s3
        region[1, 8 * t : 8 * t + 8, :] = w * parts[0]
    ws = [region[0, pl.ds(t, 8, 7), :] for t in range(7)]
    wb = [region[1, pl.ds(t, 8, 7), :] for t in range(7)]
    v = wb
    for sweep in range(NC - 1):
        top = pltpu.roll(v[6], 1, 0)
        bottom = pltpu.roll(v[0], 7, 0)
        new = []
        for t in range(7):
            up = v[t - 1] if t > 0 else top
            down = v[t + 1] if t < 6 else bottom
            near = (up + down) + (pltpu.roll(v[t], 1, 1) + pltpu.roll(v[t], 127, 1))
            new.append((0.2 * v[t] + wb[t]) + ws[t] * near)
        v = new
    for t in range(7):
        region[0, pl.ds(t, 8, 7), :] = v[t]
    coarse = jnp.concatenate(
        [region[0, 0:16, :], jnp.where(sub8 < 4, region[0, 16:24, :], region[0, 48:56, :])], axis=0
    )

    correction = [[coarse]]
    for n, s, w, wb, pre in reversed(levels):
        x = grid_of(n, lambda i, j: pre[i][j] + jnp.where(plane_in, correction[i // 2][j // 2], 0.0))
        for sweep in range(2):
            near = beside_planes(x, n)
            x = grid_of(n, lambda i, j: (0.2 * x[i][j] + wb[i][j]) + (s * w[i][j]) * near[i][j])
        correction = x
    joint = jnp.concatenate([jnp.concatenate(row_planes, axis=1) for row_planes in correction], axis=0)
    fine = matmul(joint, up_table[...])
    for kr in range(8):
        k = kr // 2
        c0 = jnp.stack([fine[24 * k : 24 * k + 24, c * 128 : (c + 1) * 128] for c in range(5)])
        put(v2, kr, v2[kr + 1] + c0)
    for kr in range(8):
        x = v2[kr + 1]
        src0[kr] = w0[kr] * src0[kr]
        put(v1, kr, (0.2 * x + src0[kr]) + w0[kr] * beside0(v2, kr))
    for kr in range(8):
        x = v1[kr + 1]
        x = (0.2 * x + src0[kr]) + w0[kr] * beside0(v1, kr)
        for c in range(4):
            out_vmem[c, pl.ds(kr, 16, 8), :] = x[c, 0:16]
    stores = [
        pltpu.make_async_copy(out_vmem.at[c], out_hbm.at[:, pl.ds(c * 128, 128)], out_sem.at[c]) for c in range(4)
    ]
    for store in stores:
        store.start()
    on_all(first, "wait_send", 1)
    on_all(second, "wait_send", 1)
    for store in stores:
        store.wait()


def solution(mesh):
    gx_size, gy_size = mesh.shape["gx"], mesh.shape["gy"]

    def per_device(right_side, kappa_field, ice_blocks):
        dma = pltpu.SemaphoreType.DMA
        return pl.pallas_call(
            functools.partial(kernel, gx_size, gy_size),
            out_shape=jax.ShapeDtypeStruct((128, 512), F32),
            in_specs=[pl.BlockSpec(memory_space=pl.ANY)] * 3,
            out_specs=pl.BlockSpec(memory_space=pl.ANY),
            scratch_shapes=[
                pltpu.VMEM((2, 5, 192, 128), F32),
                pltpu.VMEM((16, 64), jnp.int32),
                pltpu.VMEM((8, 5, 24, 128), F32),
                pltpu.VMEM((10, 5, 24, 128), F32),
                pltpu.VMEM((10, 5, 24, 128), F32),
                pltpu.VMEM((8, 5, 24, 128), F32),
                pltpu.VMEM((96, 640), F32),
                pltpu.VMEM((640, 512), BF16),
                pltpu.VMEM((512, 640), BF16),
                pltpu.VMEM((2, 2, 32, 128), F32),
                pltpu.VMEM((2, 2, 48, 128), F32),
                pltpu.VMEM((2, 24, 128), F32),
                pltpu.VMEM((8, 2, 24, 128), F32),
                pltpu.VMEM((2, 56, 128), F32),
                pltpu.VMEM((4, 128, 128), F32),
                dma((9,)), dma((4,)), dma((8,)), dma((8,)), dma((8,)), dma((8,)),
            ],
            compiler_params=pltpu.CompilerParams(
                collective_id=0, has_side_effects=True, vmem_limit_bytes=48 * 1024 * 1024
            ),
            name="v_cycle",
        )(right_side, kappa_field, ice_blocks)

    spec = P("gx", "gy")
    return jax.shard_map(per_device, mesh=mesh, in_specs=(spec,) * 3, out_specs=spec, check_vma=False)
```

time: 316 us -> 22.8 us (0.07)
  starting transfers between devices: 173 us -> 0 us
  waiting for transfers between devices: 53.6 us -> 0 us
  local copies, waits for them, and re-layouts: 53.3 us -> 3.3 us
  other arithmetic: 32.5 us -> 0 us
  Pallas kernels: 0 us -> 19.2 us
    ppermute x52 -> x0, starting transfers between devices: 173 us -> none  [the longest x20 66.1 us: with_halo(): lax.ppermute(head, axis, [((i + 1) % count, i) for i in range(ends)])]
    ppermute x52 -> x0, waiting for transfers between devices: 53.6 us -> none  [the longest x20 26.8 us: with_halo(): lax.ppermute(head, axis, [((i + 1) % count, i) for i in range(ends)])]
    reshape x10 -> x0, local copies, waits for them, and re-layouts: 43.3 us -> none  [the longest x4 42.8 us: restrict(): return field.reshape(height // 2, 2, width // 2, 2).mean(axis=(1, 3))]
    reduce_sum x6 -> x0, other arithmetic: 22.1 us -> none  [restrict(): return field.reshape(height // 2, 2, width // 2, 2).mean(axis=(1, 3))]
    pallas_call x0 -> x1, Pallas kernels: none -> 19.2 us  [per_device(): pl.pallas_call(functools.partial(kernel, gx_size, gy_size), out_shape=jax...]
    div x2 -> x0, local copies, waits for them, and re-layouts: 6.58 us -> none  [restrict(): return field.reshape(height // 2, 2, width // 2, 2).mean(axis=(1, 3))]
    mul x23 -> x0, other arithmetic: 4.07 us -> none  [the longest x6 2.61 us: deep_sweeps(): middle = jacobi_step(wider, source_rim, reaction_rim, stiffness) * keeper]
  transfers between devices with their start and end apart: 52 -> 0, of which waited for: 17 -> 0; matrix products, arithmetic and copies ran while one was open for 24% -> 0% of each run, Pallas kernels for 0% -> 0%
where the time goes in v1:
time: 22.8 us; the launch traced here: 22.5 us
  Pallas kernels  19.2 us (84%)
  local copies, waits for them, and re-layouts  3.3 us (14%)
    pallas_call x1, Pallas kernels, per_device(): pl.pallas_call(functools.partial(kernel, gx_size, gy_size), out_shape=jax...  19.2 us
    unnamed x7, local copies, waits for them, and re-layouts  3.3 us

profile of v1, /device:TPU:38, one launch (start us, length us, event | category | flops | bytes accessed | tf_op | source)
XLA Modules:
  0.0 22.5 jit_solution(6803952876700702398)
XLA Ops:
  0.0 0.0 copy-start
  0.0 0.9 %copy-done = f32[128,512]{1,0:T(8,128)S(1)} copy-done((f32[128,512]{1,0:T(8,128)S(1)}, f32[128,512]{1,0:T(8,128)}, u32[]{:S(2)}) %copy-start) | copy-done | bytes 262168
  1.0 0.0 copy-start.1
  1.0 0.9 %copy-done.1 = f32[128,512]{1,0:T(8,128)S(1)} copy-done((f32[128,512]{1,0:T(8,128)S(1)}, f32[128,512]{1,0:T(8,128)}, u32[]{:S(2)}) %copy-start.1) | copy-done | bytes 262168
  1.9 0.0 copy-start.2
  1.9 0.7 %copy-done.2 = s32[16,64]{1,0:T(8,128)S(1)} copy-done((s32[16,64]{1,0:T(8,128)S(1)}, s32[16,64]{1,0:T(8,128)}, u32[]{:S(2)}) %copy-start.2) | copy-done | bytes 4120
  2.6 19.2 %v_cycle.1 = f32[128,512]{1,0:T(8,128)S(1)} custom-call(f32[128,512]{1,0:T(8,128)S(1)} %copy-done, f32[128,512]{1,0:T(8,128)S(1)} %copy-done.1, s32[16,64]{1,0:T(8,128)S(1)} %copy-done.2), custom_call_target="tpu_custom_call" | custom-call | tf_op jit(solution)/shard_map/v_cycle/pallas_call | solution.py:379
  21.8 0.7 %copy.5 = f32[128,512]{1,0:T(8,128)} copy(f32[128,512]{1,0:T(8,128)S(1)} %v_cycle.1) | data formatting | bytes 524288
Async XLA Ops:
  0.0 0.9 %copy-start = (f32[128,512]{1,0:T(8,128)S(1)}, f32[128,512]{1,0:T(8,128)}, u32[]{:S(2)}) copy-start(f32[128,512]{1,0:T(8,128)} %rs_hbm.1) | copy-start | bytes 786436
  1.0 0.9 %copy-start.1 = (f32[128,512]{1,0:T(8,128)S(1)}, f32[128,512]{1,0:T(8,128)}, u32[]{:S(2)}) copy-start(f32[128,512]{1,0:T(8,128)} %kappa_hbm.1) | copy-start | bytes 786436
  1.9 0.7 %copy-start.2 = (s32[16,64]{1,0:T(8,128)S(1)}, s32[16,64]{1,0:T(8,128)}, u32[]{:S(2)}) copy-start(s32[16,64]{1,0:T(8,128)} %ice_hbm.1) | copy-start | bytes 12292

commit v2 on v1

v2 whole, which is shorter than its diff:
```python
import functools

import jax
import jax.numpy as jnp
from jax import lax
from jax.experimental import pallas as pl
from jax.experimental.pallas import tpu as pltpu
from jax.sharding import PartitionSpec as P

MESH = pl.DeviceIdType.MESH
F32 = jnp.float32
BF16 = jnp.bfloat16
NC = 16
DAMP = 0.8


DIRS = ((-1, -1), (-1, 1), (1, -1), (1, 1), (0, -1), (0, 1), (-1, 0), (1, 0))


def lanes_of(shape):
    return lax.broadcasted_iota(jnp.int32, shape, len(shape) - 1)


def rows_of(shape):
    return lax.broadcasted_iota(jnp.int32, shape, len(shape) - 2)


def split(x):
    high = x.astype(BF16)
    low = (x - high.astype(F32)).astype(BF16)
    return high, low


def matmul(x, table):
    high, low = split(x)
    return jnp.dot(high, table, preferred_element_type=F32) + jnp.dot(low, table, preferred_element_type=F32)


def side_sum_0(x, lane):
    a = pltpu.roll(x, 1, 2)
    b = pltpu.roll(x, 127, 2)
    left = jnp.where(lane == 0, jnp.concatenate([a[-1:], a[:-1]], axis=0), a)
    right = jnp.where(lane == 127, jnp.concatenate([b[1:], b[:1]], axis=0), b)
    return left + right


def beside_planes(v, count):
    out = []
    last = v[0][0].shape[0] - 1
    for kr in range(count):
        row = []
        for kc in range(count):
            up = v[kr - 1][kc] if kr > 0 else pltpu.roll(v[count - 1][kc], 1, 0)
            down = v[kr + 1][kc] if kr < count - 1 else pltpu.roll(v[0][kc], last, 0)
            left = v[kr][kc - 1] if kc > 0 else pltpu.roll(v[kr][count - 1], 1, 1)
            right = v[kr][kc + 1] if kc < count - 1 else pltpu.roll(v[kr][0], 127, 1)
            row.append((up + down) + (left + right))
        out.append(row)
    return out


def kernel(
    gx_size, gy_size,
    rs_hbm, kappa_hbm, ice_hbm, out_ref,
    field, ice, w0, v1, v2, src0, early2, lhs, down_table, up_table, snd, rcv, t3, rb, t3_early, rb_early, region,
    out_vmem, local_sem, ssem1, rsem1, ssem2, rsem2,
):
    gx = lax.axis_index("gx")
    gy = lax.axis_index("gy")

    def there(dx, dy):
        return (gx + dx >= 0) & (gx + dx < gx_size) & (gy + dy >= 0) & (gy + dy < gy_size)

    barrier = pltpu.get_barrier_semaphore()
    count = jnp.int32(0)
    for dx, dy in DIRS:
        here = there(dx, dy)
        count = count + here.astype(jnp.int32)

        @pl.when(here)
        def _():
            pl.semaphore_signal(barrier, inc=1, device_id=(gx + dx, gy + dy), device_id_type=MESH)

    loads = [pltpu.make_async_copy(ice_hbm, ice, local_sem.at[8])]
    for c in (0, 3, 1, 2):
        for a, ref in ((1, kappa_hbm), (0, rs_hbm)):
            loads.append(
                pltpu.make_async_copy(
                    ref.at[:, pl.ds(c * 128, 128)], field.at[a, c, pl.ds(0, 128), :], local_sem.at[a * 4 + c]
                )
            )
    for load in loads:
        load.start()

    @pl.when(gx == 0)
    def _():
        field[:, 0:4, 160:192, :] = jnp.zeros((2, 4, 32, 128), F32)
        rcv[:, :, 80:96, :] = jnp.zeros((2, 2, 16, 128), F32)

    @pl.when(gx == gx_size - 1)
    def _():
        field[:, 0:4, 128:160, :] = jnp.zeros((2, 4, 32, 128), F32)
        rcv[:, :, 64:80, :] = jnp.zeros((2, 2, 16, 128), F32)

    @pl.when(gy == 0)
    def _():
        rcv[0] = jnp.zeros((2, 96, 128), F32)

    @pl.when(gy == gy_size - 1)
    def _():
        rcv[1] = jnp.zeros((2, 96, 128), F32)

    for i, (dx, dy) in enumerate(DIRS):
        @pl.when(jnp.logical_not(there(-dx, -dy)))
        def _():
            if i < 4:
                rb_early[i] = jnp.zeros((2, 16, 128), F32)
            else:
                rb[i - 4] = jnp.zeros((2, 24, 128), F32)

    loads[0].wait()
    spread = lax.broadcasted_iota(jnp.int32, (64, 512), 0) == (lax.broadcasted_iota(jnp.int32, (64, 512), 1) >> 3)
    wide = jnp.dot(
        ice[...].astype(F32).astype(BF16), jnp.where(spread, 1.0, 0.0).astype(BF16), preferred_element_type=F32
    )
    factor = 1.0 + 3.0 * (1.0 - wide)
    for load in loads[1:]:
        load.wait()

    def react(c, tile, tiles):
        rows = slice(8 * tile, 8 * (tile + tiles))
        own = field[1, c, rows, :].reshape(tiles, 8, 128) * factor[
            tile : tile + tiles, c * 128 : (c + 1) * 128
        ].reshape(tiles, 1, 128)
        field[1, c, rows, :] = own.reshape(8 * tiles, 128)

    for c in (0, 3):
        react(c, 0, 16)
    for c in (1, 2):
        react(c, 0, 4)
        react(c, 12, 4)

    low8 = lanes_of((8, 128)) < 64
    for a in range(2):
        for tt in range(8):
            top = pl.ds(16 * tt, 8)
            bottom = pl.ds(16 * tt + 8, 8)
            snd[0, a, pl.ds(8 * tt, 8), :] = jnp.where(low8, pltpu.roll(field[a, 3, top, :], 64, 1), field[a, 3, bottom, :])
            snd[1, a, pl.ds(8 * tt, 8), :] = jnp.where(low8, field[a, 0, top, :], pltpu.roll(field[a, 0, bottom, :], 64, 1))

    pl.semaphore_wait(barrier, count)

    def first(i):
        dx, dy = DIRS[i]
        if dy == 0:
            src = field.at[:, pl.ds(0, 4), pl.ds(0 if dx < 0 else 96, 32), :]
            dst = field.at[:, pl.ds(0, 4), pl.ds(128 if dx < 0 else 160, 32), :]
        elif dx == 0:
            side = 0 if dy > 0 else 1
            src = snd.at[side]
            dst = rcv.at[side, :, pl.ds(0, 64), :]
        else:
            side = 0 if dy > 0 else 1
            src = snd.at[side, :, pl.ds(0 if dx < 0 else 48, 16), :]
            dst = rcv.at[side, :, pl.ds(64 if dx < 0 else 80, 16), :]
        return pltpu.make_async_remote_copy(
            src_ref=src, dst_ref=dst, send_sem=ssem1.at[i], recv_sem=rsem1.at[i],
            device_id=(gx + dx, gy + dy), device_id_type=MESH,
        )

    def early(i):
        dx, dy = DIRS[i]
        return pltpu.make_async_remote_copy(
            src_ref=t3_early, dst_ref=rb_early.at[i], send_sem=ssem2.at[i], recv_sem=rsem2.at[i],
            device_id=(gx + dx, gy + dy), device_id_type=MESH,
        )

    def second(i):
        dx, dy = DIRS[i]
        return pltpu.make_async_remote_copy(
            src_ref=t3, dst_ref=rb.at[i - 4], send_sem=ssem2.at[i], recv_sem=rsem2.at[i],
            device_id=(gx + dx, gy + dy), device_id_type=MESH,
        )

    def on_all(make, action, sign, part=range(8)):
        for i in part:
            dx, dy = DIRS[i]

            @pl.when(there(sign * dx, sign * dy))
            def _():
                getattr(make(i), action)()

    corners, sides = range(4), range(4, 8)

    on_all(first, "start", 1)

    fine = lax.broadcasted_iota(jnp.int32, (640, 512), 0)
    col = jnp.where(fine >= 576, fine - 640, fine)
    plane_lane = lax.broadcasted_iota(jnp.int32, (640, 512), 1)
    target = 8 * ((plane_lane & 127) - 32) + 2 * (plane_lane >> 7)
    near = (col & -2) == target
    down_table[...] = jnp.where(near, 0.25, 0.0).astype(BF16)
    fine = lax.broadcasted_iota(jnp.int32, (512, 640), 1)
    col = jnp.where(fine >= 576, fine - 640, fine)
    plane_lane = lax.broadcasted_iota(jnp.int32, (512, 640), 0)
    target = 8 * ((plane_lane & 127) - 32) + 2 * (plane_lane >> 7)
    near = (col & -2) == target
    up_table[...] = jnp.where(near, 1.0, 0.0).astype(BF16)

    for c in (1, 2):
        react(c, 4, 8)

    def cut(x, n):
        rows = x.shape[0] // n
        return [[x[rows * i : rows * i + rows, 128 * j : 128 * j + 128] for j in range(n)] for i in range(n)]

    def coarsen(x, n):
        return [
            [
                0.25 * ((x[2 * i][2 * j] + x[2 * i + 1][2 * j]) + (x[2 * i][2 * j + 1] + x[2 * i + 1][2 * j + 1]))
                for j in range(n)
            ]
            for i in range(n)
        ]

    def grid_of(n, make):
        return [[make(i, j) for j in range(n)] for i in range(n)]

    def down(source, reaction, inside):
        levels = []
        for level, n in ((1, 4), (2, 2)):
            s = 0.25**level
            d = grid_of(n, lambda i, j: reaction[i][j] + 4.0 * s)
            w = grid_of(n, lambda i, j: DAMP / d[i][j])
            if inside is not None:
                w = grid_of(n, lambda i, j: jnp.where(inside, w[i][j], 0.0))
            wb = grid_of(n, lambda i, j: w[i][j] * source[i][j])
            near1 = beside_planes(wb, n)
            pre = grid_of(n, lambda i, j: 1.2 * wb[i][j] + (s * w[i][j]) * near1[i][j])
            near2 = beside_planes(pre, n)
            rest = grid_of(n, lambda i, j: (source[i][j] - d[i][j] * pre[i][j]) + s * near2[i][j])
            levels.append((n, s, w, wb, pre))
            source, reaction = coarsen(rest, n // 2), coarsen(reaction, n // 2)
        return source[0][0], reaction[0][0], levels

    lane4 = lanes_of((4, 16, 128))

    def fold(rows, tiles, kr, x, pair):
        if kr % 2 == 0:
            return x
        x = x + pair
        for c in range(tiles):
            lhs[rows * (kr // 2) : rows * (kr // 2 + 1), c * 128 : (c + 1) * 128] = x[c]
        return None

    def own(ref, kr):
        if kr == -1:
            return pltpu.roll(ref[8, 0:4, 0:16, :], 1, 1)
        if kr == 8:
            return pltpu.roll(ref[1, 0:4, 0:16, :], 15, 1)
        return ref[kr + 1, 0:4, 0:16, :]

    def beside_own(ref, kr):
        return (own(ref, kr - 1) + own(ref, kr + 1)) + side_sum_0(own(ref, kr), lane4)

    def own_planes(a, kr):
        return jnp.stack([field[a, c, pl.ds(kr, 16, 8), :] for c in range(4)])

    pair = None
    for kr in range(8):
        r = own_planes(1, kr)
        b = own_planes(0, kr)
        w = DAMP / (r + 4.0)
        w0[kr, 0:4, 0:16, :] = w
        src0[kr, 0:4, 0:16, :] = b
        v1[kr + 1, 0:4, 0:16, :] = w * b
        pair = fold(16, 4, kr, r, pair)
    reaction1 = matmul(lhs[0:64, 0:512], down_table[0:512, :])
    for kr in range(8):
        early2[kr + 1, 0:4, 0:16, :] = 1.2 * own(v1, kr) + w0[kr, 0:4, 0:16, :] * beside_own(v1, kr)
    for kr in range(8):
        r = own_planes(1, kr)
        rest = (src0[kr, 0:4, 0:16, :] - (r + 4.0) * own(early2, kr)) + beside_own(early2, kr)
        pair = fold(16, 4, kr, rest, pair)
    source1 = matmul(lhs[0:64, 0:512], down_table[0:512, :])
    t3_early[0], t3_early[1], _ = down(cut(source1, 4), cut(reaction1, 4), None)
    on_all(early, "start", 1, corners)

    on_all(first, "wait_recv", -1)

    for a in range(2):
        for tt in range(12):
            from_left = rcv[0, a, 8 * tt : 8 * tt + 8, :]
            from_right = rcv[1, a, 8 * tt : 8 * tt + 8, :]
            turned = pltpu.roll(jnp.where(low8, from_left, from_right), 64, 1)
            field[a, 4, 16 * tt : 16 * tt + 8, :] = jnp.where(low8, from_right, turned)
            field[a, 4, 16 * tt + 8 : 16 * tt + 16, :] = jnp.where(low8, turned, from_left)

    row = rows_of((24, 128))
    lane = lanes_of((24, 128))
    row_in = ((row < 16) | ((row < 20) & (gx < gx_size - 1))) | ((row >= 20) & (gx > 0))
    right_in = gy < gy_size - 1
    left_in = gy > 0
    tile_in = row_in & (((lane < 64) & right_in) | ((lane >= 64) & left_in))
    plane_in = row_in & (((lane >= 32) & (lane < 96)) | ((lane >= 96) & right_in) | ((lane < 32) & left_in))
    lane5 = lanes_of((5, 24, 128))

    def reactions(kr):
        return jnp.stack([field[1, c, pl.ds(kr, 24, 8), :] for c in range(5)])

    def put(ref, kr, x):
        ref[kr + 1] = x
        if kr == 7:
            ref[0] = pltpu.roll(x, 1, 1)
        if kr == 0:
            ref[9] = pltpu.roll(x, 23, 1)

    def beside0(ref, kr):
        return (ref[kr] + ref[kr + 2]) + side_sum_0(ref[kr + 1], lane5)

    halo_in = row_in[16:24, :]
    pair = None
    for kr in range(8):
        tile_r = field[1, 4, pl.ds(kr, 24, 8), :]
        tile_b = field[0, 4, pl.ds(kr, 24, 8), :]
        halo_r = jnp.stack([field[1, c, pl.ds(128 + kr, 8, 8), :] for c in range(4)])
        halo_b = jnp.stack([field[0, c, pl.ds(128 + kr, 8, 8), :] for c in range(4)])
        tile_w = jnp.where(tile_in, DAMP / (tile_r + 4.0), 0.0)
        halo_w = jnp.where(halo_in, DAMP / (halo_r + 4.0), 0.0)
        w0[kr, 4] = tile_w
        w0[kr, 0:4, 16:24, :] = halo_w
        src0[kr, 4] = tile_b
        src0[kr, 0:4, 16:24, :] = halo_b
        v1[kr + 1, 4] = tile_w * tile_b
        v1[kr + 1, 0:4, 16:24, :] = halo_w * halo_b
        pair = fold(24, 5, kr, reactions(kr), pair)
    v1[0] = pltpu.roll(v1[8], 1, 1)
    v1[9] = pltpu.roll(v1[1], 23, 1)
    reaction1 = matmul(lhs[...], down_table[...])
    for kr in range(8):
        put(v2, kr, 1.2 * v1[kr + 1] + w0[kr] * beside0(v1, kr))
    for kr in range(8):
        rest = (src0[kr] - (reactions(kr) + 4.0) * v2[kr + 1]) + beside0(v2, kr)
        pair = fold(24, 5, kr, rest, pair)
    source1 = matmul(lhs[...], down_table[...])

    source3, reaction3, levels = down(cut(source1, 4), cut(reaction1, 4), plane_in)

    t3[0] = source3
    t3[1] = reaction3
    on_all(second, "start", 1, sides)
    on_all(second, "wait_recv", -1, sides)
    on_all(early, "wait_recv", -1, corners)

    lane8 = lanes_of((8, 128))
    sub8 = rows_of((8, 128))
    own8 = (lane8 >= 29) & (lane8 < 99)
    high8 = lane8 >= 64

    def arrived(dx, dy):
        return rb.at[DIRS.index((-dx, -dy)) - 4]

    def corner(a, dx, dy, start):
        x = rb_early[DIRS.index((-dx, -dy)), a, start : start + 8, :]
        if dx < 0 and start == 8:
            return jnp.where(sub8 >= 6, arrived(0, dy)[a, 16:24, :], x)
        if dx > 0 and start == 0:
            return jnp.where(sub8 < 2, arrived(0, dy)[a, 16:24, :], x)
        return x

    def joined(a, dx, start):
        if dx == 0:
            middle = t3[a, start : start + 8, :]
            left, right = (arrived(0, dy)[a, start : start + 8, :] for dy in (-1, 1))
        else:
            middle = arrived(dx, 0)[a, start : start + 8, :]
            left, right = (corner(a, dx, dy, start) for dy in (-1, 1))
        return jnp.where(own8, middle, pltpu.roll(jnp.where(high8, left, right), 64, 1))

    s3 = 0.25**3
    for t in range(7):
        if t == 4:
            parts = [jnp.where(sub8 == 7, arrived(-1, 0)[a, 16:24, :], arrived(1, 0)[a, 16:24, :]) for a in range(2)]
        else:
            dx, start = ((0, 0), (0, 8), (1, 0), (1, 8), None, (-1, 0), (-1, 8))[t]
            parts = [joined(a, dx, start) for a in range(2)]
        spot = 8 * t + sub8
        spot = jnp.where(spot >= 36, spot - 56, spot) + 16 * gx
        side = lane8 - 32 + 64 * gy
        inside = (spot >= 0) & (spot < 16 * gx_size) & (side >= 0) & (side < 64 * gy_size)
        w = jnp.where(inside, DAMP / (parts[1] + 4.0 * s3), 0.0)
        region[0, 8 * t : 8 * t + 8, :] = w * s3
        region[1, 8 * t : 8 * t + 8, :] = w * parts[0]
    ws = [region[0, pl.ds(t, 8, 7), :] for t in range(7)]
    wb = [region[1, pl.ds(t, 8, 7), :] for t in range(7)]
    v = wb
    for sweep in range(NC - 1):
        top = pltpu.roll(v[6], 1, 0)
        bottom = pltpu.roll(v[0], 7, 0)
        new = []
        for t in range(7):
            up = v[t - 1] if t > 0 else top
            down = v[t + 1] if t < 6 else bottom
            near = (up + down) + (pltpu.roll(v[t], 1, 1) + pltpu.roll(v[t], 127, 1))
            new.append((0.2 * v[t] + wb[t]) + ws[t] * near)
        v = new
    for t in range(7):
        region[0, pl.ds(t, 8, 7), :] = v[t]
    coarse = jnp.concatenate(
        [region[0, 0:16, :], jnp.where(sub8 < 4, region[0, 16:24, :], region[0, 48:56, :])], axis=0
    )

    correction = [[coarse]]
    for n, s, w, wb, pre in reversed(levels):
        x = grid_of(n, lambda i, j: pre[i][j] + jnp.where(plane_in, correction[i // 2][j // 2], 0.0))
        for sweep in range(2):
            near = beside_planes(x, n)
            x = grid_of(n, lambda i, j: (0.2 * x[i][j] + wb[i][j]) + (s * w[i][j]) * near[i][j])
        correction = x
    joint = jnp.concatenate([jnp.concatenate(row_planes, axis=1) for row_planes in correction], axis=0)
    fine = matmul(joint, up_table[...])
    for kr in range(8):
        k = kr // 2
        c0 = jnp.stack([fine[24 * k : 24 * k + 24, c * 128 : (c + 1) * 128] for c in range(5)])
        put(v2, kr, v2[kr + 1] + c0)
    for kr in range(8):
        x = v2[kr + 1]
        src0[kr] = w0[kr] * src0[kr]
        put(v1, kr, (0.2 * x + src0[kr]) + w0[kr] * beside0(v2, kr))
    for kr in range(8):
        x = v1[kr + 1]
        x = (0.2 * x + src0[kr]) + w0[kr] * beside0(v1, kr)
        for c in range(4):
            out_vmem[c, pl.ds(kr, 16, 8), :] = x[c, 0:16]
    for c in range(4):
        out_ref[:, c * 128 : (c + 1) * 128] = out_vmem[c]
    on_all(first, "wait_send", 1)
    on_all(early, "wait_send", 1, corners)
    on_all(second, "wait_send", 1, sides)


def solution(mesh):
    gx_size, gy_size = mesh.shape["gx"], mesh.shape["gy"]

    def per_device(right_side, kappa_field, ice_blocks):
        dma = pltpu.SemaphoreType.DMA
        return pl.pallas_call(
            functools.partial(kernel, gx_size, gy_size),
            out_shape=pltpu.VMEM((128, 512), F32),
            in_specs=[pl.BlockSpec(memory_space=pltpu.HBM)] * 3,
            out_specs=pl.BlockSpec(memory_space=pltpu.VMEM),
            scratch_shapes=[
                pltpu.VMEM((2, 5, 192, 128), F32),
                pltpu.VMEM((16, 64), jnp.int32),
                pltpu.VMEM((8, 5, 24, 128), F32),
                pltpu.VMEM((10, 5, 24, 128), F32),
                pltpu.VMEM((10, 5, 24, 128), F32),
                pltpu.VMEM((8, 5, 24, 128), F32),
                pltpu.VMEM((10, 4, 16, 128), F32),
                pltpu.VMEM((96, 640), F32),
                pltpu.VMEM((640, 512), BF16),
                pltpu.VMEM((512, 640), BF16),
                pltpu.VMEM((2, 2, 64, 128), F32),
                pltpu.VMEM((2, 2, 96, 128), F32),
                pltpu.VMEM((2, 24, 128), F32),
                pltpu.VMEM((4, 2, 24, 128), F32),
                pltpu.VMEM((2, 16, 128), F32),
                pltpu.VMEM((4, 2, 16, 128), F32),
                pltpu.VMEM((2, 56, 128), F32),
                pltpu.VMEM((4, 128, 128), F32),
                dma((9,)), dma((8,)), dma((8,)), dma((8,)), dma((8,)),
            ],
            compiler_params=pltpu.CompilerParams(
                collective_id=0, has_side_effects=True, vmem_limit_bytes=60 * 1024 * 1024
            ),
            name="v_cycle",
        )(right_side, kappa_field, ice_blocks)

    spec = P("gx", "gy")
    return jax.shard_map(per_device, mesh=mesh, in_specs=(spec,) * 3, out_specs=spec, check_vma=False)
```

time: 22.8 us -> 18.5 us (0.81)
  local copies, waits for them, and re-layouts: 3.3 us -> 0.71 us
  Pallas kernels: 19.2 us -> 17.7 us
    unnamed x7 -> x1, local copies, waits for them, and re-layouts: 3.3 us -> 0.71 us
    pallas_call x1, Pallas kernels: 19.2 us -> 17.7 us  [per_device(): pl.pallas_call(functools.partial(kernel, gx_size, gy_size), out_shape=plt...]
where the time goes in v2:
time: 18.5 us; the launch traced here: 18.4 us
  Pallas kernels  17.7 us (96%)
  local copies, waits for them, and re-layouts  0.71 us (4%)
    pallas_call x1, Pallas kernels, per_device(): pl.pallas_call(functools.partial(kernel, gx_size, gy_size), out_shape=plt...  17.7 us
    unnamed x1, local copies, waits for them, and re-layouts  0.71 us

profile of v2, /device:TPU:38, one launch (start us, length us, event | category | flops | bytes accessed | tf_op | source)
XLA Modules:
  0.0 18.4 jit_solution(75260300766564704)
XLA Ops:
  0.0 17.7 %v_cycle.1 = f32[128,512]{1,0:T(8,128)S(1)} custom-call(f32[128,512]{1,0:T(8,128)} %rs_hbm.1, f32[128,512]{1,0:T(8,128)} %kappa_hbm.1, s32[16,64]{1,0:T(8,128)} %ice_hbm.1), custom_call_target="tpu_custom_call" | custom-call | tf_op jit(solution)/shard_map/v_cycle/pallas_call | solution.py:447
  17.7 0.7 %copy.5 = f32[128,512]{1,0:T(8,128)} copy(f32[128,512]{1,0:T(8,128)S(1)} %v_cycle.1) | data formatting | bytes 524288

commit v3 on v2

--- a/solution.py
+++ b/solution.py
@@ -44,25 +44,29 @@
     return left + right
 
 
-def beside_planes(v, count):
+def extended(v, width):
+    n = len(v)
     out = []
-    last = v[0][0].shape[0] - 1
-    for kr in range(count):
-        row = []
-        for kc in range(count):
-            up = v[kr - 1][kc] if kr > 0 else pltpu.roll(v[count - 1][kc], 1, 0)
-            down = v[kr + 1][kc] if kr < count - 1 else pltpu.roll(v[0][kc], last, 0)
-            left = v[kr][kc - 1] if kc > 0 else pltpu.roll(v[kr][count - 1], 1, 1)
-            right = v[kr][kc + 1] if kc < count - 1 else pltpu.roll(v[kr][0], 127, 1)
-            row.append((up + down) + (left + right))
-        out.append(row)
+    for row in v:
+        wide = dict(enumerate(row))
+        for k in range(1, width + 1):
+            wide[-k] = pltpu.roll(row[n - k], 1, 1)
+            wide[n - 1 + k] = pltpu.roll(row[k - 1], 127, 1)
+        out.append(wide)
     return out
+
+
+def beside_planes(v, kr, kc):
+    n, last = len(v), v[0][0].shape[0] - 1
+    up = v[kr - 1][kc] if kr > 0 else pltpu.roll(v[n - 1][kc], 1, 0)
+    down = v[kr + 1][kc] if kr < n - 1 else pltpu.roll(v[0][kc], last, 0)
+    return (up + down) + (v[kr][kc - 1] + v[kr][kc + 1])
 
 
 def kernel(
     gx_size, gy_size,
     rs_hbm, kappa_hbm, ice_hbm, out_ref,
-    field, ice, w0, v1, v2, src0, early2, lhs, down_table, up_table, snd, rcv, t3, rb, t3_early, rb_early, region,
+    field, ice, w0, v1, v2, src0, r0, early2, lhs, down_table, up_table, snd, rcv, t3, rb, t3_early, rb_early, region,
     out_vmem, local_sem, ssem1, rsem1, ssem2, rsem2,
 ):
     gx = lax.axis_index("gx")
@@ -226,6 +230,9 @@
     def grid_of(n, make):
         return [[make(i, j) for j in range(n)] for i in range(n)]
 
+    def wide_of(n, make):
+        return [{j: make(i, j) for j in range(-1, n + 1)} for i in range(n)]
+
     def down(source, reaction, inside):
         levels = []
         for level, n in ((1, 4), (2, 2)):
@@ -234,12 +241,11 @@
             w = grid_of(n, lambda i, j: DAMP / d[i][j])
             if inside is not None:
                 w = grid_of(n, lambda i, j: jnp.where(inside, w[i][j], 0.0))
-            wb = grid_of(n, lambda i, j: w[i][j] * source[i][j])
-            near1 = beside_planes(wb, n)
-            pre = grid_of(n, lambda i, j: 1.2 * wb[i][j] + (s * w[i][j]) * near1[i][j])
-            near2 = beside_planes(pre, n)
-            rest = grid_of(n, lambda i, j: (source[i][j] - d[i][j] * pre[i][j]) + s * near2[i][j])
-            levels.append((n, s, w, wb, pre))
+            wb = extended(grid_of(n, lambda i, j: w[i][j] * source[i][j]), 2)
+            sw = extended(grid_of(n, lambda i, j: s * w[i][j]), 1)
+            pre = wide_of(n, lambda i, j: 1.2 * wb[i][j] + sw[i][j] * beside_planes(wb, i, j))
+            rest = grid_of(n, lambda i, j: (source[i][j] - d[i][j] * pre[i][j]) + s * beside_planes(pre, i, j))
+            levels.append((n, sw, wb, pre))
             source, reaction = coarsen(rest, n // 2), coarsen(reaction, n // 2)
         return source[0][0], reaction[0][0], levels
 
@@ -273,13 +279,14 @@
         w = DAMP / (r + 4.0)
         w0[kr, 0:4, 0:16, :] = w
         src0[kr, 0:4, 0:16, :] = b
+        r0[kr, 0:4, 0:16, :] = r
         v1[kr + 1, 0:4, 0:16, :] = w * b
         pair = fold(16, 4, kr, r, pair)
     reaction1 = matmul(lhs[0:64, 0:512], down_table[0:512, :])
     for kr in range(8):
         early2[kr + 1, 0:4, 0:16, :] = 1.2 * own(v1, kr) + w0[kr, 0:4, 0:16, :] * beside_own(v1, kr)
     for kr in range(8):
-        r = own_planes(1, kr)
+        r = r0[kr, 0:4, 0:16, :]
         rest = (src0[kr, 0:4, 0:16, :] - (r + 4.0) * own(early2, kr)) + beside_own(early2, kr)
         pair = fold(16, 4, kr, rest, pair)
     source1 = matmul(lhs[0:64, 0:512], down_table[0:512, :])
@@ -305,9 +312,6 @@
     plane_in = row_in & (((lane >= 32) & (lane < 96)) | ((lane >= 96) & right_in) | ((lane < 32) & left_in))
     lane5 = lanes_of((5, 24, 128))
 
-    def reactions(kr):
-        return jnp.stack([field[1, c, pl.ds(kr, 24, 8), :] for c in range(5)])
-
     def put(ref, kr, x):
         ref[kr + 1] = x
         if kr == 7:
@@ -327,20 +331,22 @@
         halo_b = jnp.stack([field[0, c, pl.ds(128 + kr, 8, 8), :] for c in range(4)])
         tile_w = jnp.where(tile_in, DAMP / (tile_r + 4.0), 0.0)
         halo_w = jnp.where(halo_in, DAMP / (halo_r + 4.0), 0.0)
+        r0[kr, 4] = tile_r
+        r0[kr, 0:4, 16:24, :] = halo_r
         w0[kr, 4] = tile_w
         w0[kr, 0:4, 16:24, :] = halo_w
         src0[kr, 4] = tile_b
         src0[kr, 0:4, 16:24, :] = halo_b
         v1[kr + 1, 4] = tile_w * tile_b
         v1[kr + 1, 0:4, 16:24, :] = halo_w * halo_b
-        pair = fold(24, 5, kr, reactions(kr), pair)
+        pair = fold(24, 5, kr, r0[kr], pair)
     v1[0] = pltpu.roll(v1[8], 1, 1)
     v1[9] = pltpu.roll(v1[1], 23, 1)
     reaction1 = matmul(lhs[...], down_table[...])
     for kr in range(8):
         put(v2, kr, 1.2 * v1[kr + 1] + w0[kr] * beside0(v1, kr))
     for kr in range(8):
-        rest = (src0[kr] - (reactions(kr) + 4.0) * v2[kr + 1]) + beside0(v2, kr)
+        rest = (src0[kr] - (r0[kr] + 4.0) * v2[kr + 1]) + beside0(v2, kr)
         pair = fold(24, 5, kr, rest, pair)
     source1 = matmul(lhs[...], down_table[...])
 
@@ -391,19 +397,36 @@
         w = jnp.where(inside, DAMP / (parts[1] + 4.0 * s3), 0.0)
         region[0, 8 * t : 8 * t + 8, :] = w * s3
         region[1, 8 * t : 8 * t + 8, :] = w * parts[0]
-    ws = [region[0, pl.ds(t, 8, 7), :] for t in range(7)]
-    wb = [region[1, pl.ds(t, 8, 7), :] for t in range(7)]
-    v = wb
-    for sweep in range(NC - 1):
-        top = pltpu.roll(v[6], 1, 0)
-        bottom = pltpu.roll(v[0], 7, 0)
-        new = []
-        for t in range(7):
-            up = v[t - 1] if t > 0 else top
-            down = v[t + 1] if t < 6 else bottom
-            near = (up + down) + (pltpu.roll(v[t], 1, 1) + pltpu.roll(v[t], 127, 1))
-            new.append((0.2 * v[t] + wb[t]) + ws[t] * near)
-        v = new
+    def tiles_around(x, width):
+        if width == 0:
+            return x
+        return jnp.concatenate([pltpu.roll(x[7 - width :], 1, 1), x, pltpu.roll(x[:width], 7, 1)], axis=0)
+
+    def turned(x, reach):
+        return {
+            k: tiles_around(pltpu.roll(x, k % 128, 2) if k else x, reach - abs(k)) for k in range(-reach, reach + 1)
+        }
+
+    def inner(x, count):
+        return x[count : x.shape[0] - count]
+
+    ws = turned(jnp.stack([region[0, pl.ds(t, 8, 7), :] for t in range(7)]), 2)
+    wb = turned(jnp.stack([region[1, pl.ds(t, 8, 7), :] for t in range(7)]), 2)
+    v = wb[0][2:9]
+    for group in range((NC - 1) // 3):
+        x = turned(v, 3)
+        for reach in (2, 1, 0):
+            new = {}
+            for k in range(-reach, reach + 1):
+                m = reach - abs(k)
+                trim = 2 - abs(k) - m
+                mid = x[k]
+                low = (x[k - 1].shape[0] - 7) // 2 - m
+                high = (x[k + 1].shape[0] - 7) // 2 - m
+                near = (mid[:-2] + mid[2:]) + (inner(x[k - 1], low) + inner(x[k + 1], high))
+                new[k] = (0.2 * mid[1:-1] + inner(wb[k], trim)) + inner(ws[k], trim) * near
+            x = new
+        v = x[0]
     for t in range(7):
         region[0, pl.ds(t, 8, 7), :] = v[t]
     coarse = jnp.concatenate(
@@ -411,12 +434,10 @@
     )
 
     correction = [[coarse]]
-    for n, s, w, wb, pre in reversed(levels):
-        x = grid_of(n, lambda i, j: pre[i][j] + jnp.where(plane_in, correction[i // 2][j // 2], 0.0))
-        for sweep in range(2):
-            near = beside_planes(x, n)
-            x = grid_of(n, lambda i, j: (0.2 * x[i][j] + wb[i][j]) + (s * w[i][j]) * near[i][j])
-        correction = x
+    for n, sw, wb, pre in reversed(levels):
+        x = extended(grid_of(n, lambda i, j: pre[i][j] + jnp.where(plane_in, correction[i // 2][j // 2], 0.0)), 2)
+        once = wide_of(n, lambda i, j: (0.2 * x[i][j] + wb[i][j]) + sw[i][j] * beside_planes(x, i, j))
+        correction = grid_of(n, lambda i, j: (0.2 * once[i][j] + wb[i][j]) + sw[i][j] * beside_planes(once, i, j))
     joint = jnp.concatenate([jnp.concatenate(row_planes, axis=1) for row_planes in correction], axis=0)
     fine = matmul(joint, up_table[...])
     for kr in range(8):
@@ -455,6 +476,7 @@
                 pltpu.VMEM((8, 5, 24, 128), F32),
                 pltpu.VMEM((10, 5, 24, 128), F32),
                 pltpu.VMEM((10, 5, 24, 128), F32),
+                pltpu.VMEM((8, 5, 24, 128), F32),
                 pltpu.VMEM((8, 5, 24, 128), F32),
                 pltpu.VMEM((10, 4, 16, 128), F32),
                 pltpu.VMEM((96, 640), F32),

time: 18.5 us -> 18 us (0.973)
  Pallas kernels: 17.7 us -> 17.2 us
    pallas_call x1, Pallas kernels: 17.7 us -> 17.2 us  [per_device(): pl.pallas_call(functools.partial(kernel, gx_size, gy_size), out_shape=plt...]
where the time goes in v3:
time: 18 us; the launch traced here: 17.9 us
  Pallas kernels  17.2 us (96%)
  local copies, waits for them, and re-layouts  0.71 us (4%)
    pallas_call x1, Pallas kernels, per_device(): pl.pallas_call(functools.partial(kernel, gx_size, gy_size), out_shape=plt...  17.2 us
    unnamed x1, local copies, waits for them, and re-layouts  0.71 us

profile of v3, /device:TPU:38, one launch (start us, length us, event | category | flops | bytes accessed | tf_op | source)
XLA Modules:
  0.0 17.9 jit_solution(11241664571392068127)
XLA Ops:
  0.0 17.2 %v_cycle.1 = f32[128,512]{1,0:T(8,128)S(1)} custom-call(f32[128,512]{1,0:T(8,128)} %rs_hbm.1, f32[128,512]{1,0:T(8,128)} %kappa_hbm.1, s32[16,64]{1,0:T(8,128)} %ice_hbm.1), custom_call_target="tpu_custom_call" | custom-call | tf_op jit(solution)/shard_map/v_cycle/pallas_call | solution.py:468
  17.2 0.7 %copy.5 = f32[128,512]{1,0:T(8,128)} copy(f32[128,512]{1,0:T(8,128)S(1)} %v_cycle.1) | data formatting | bytes 524288

commit v4 on v3

--- a/solution.py
+++ b/solution.py
@@ -67,7 +67,7 @@
     gx_size, gy_size,
     rs_hbm, kappa_hbm, ice_hbm, out_ref,
     field, ice, w0, v1, v2, src0, r0, early2, lhs, down_table, up_table, snd, rcv, t3, rb, t3_early, rb_early, region,
-    out_vmem, local_sem, ssem1, rsem1, ssem2, rsem2,
+    out_vmem, local_sem, ssem1, rsem1, ssem2, rsem2, ssem3, rsem3,
 ):
     gx = lax.axis_index("gx")
     gy = lax.axis_index("gy")
@@ -117,10 +117,9 @@
     for i, (dx, dy) in enumerate(DIRS):
         @pl.when(jnp.logical_not(there(-dx, -dy)))
         def _():
-            if i < 4:
-                rb_early[i] = jnp.zeros((2, 16, 128), F32)
-            else:
-                rb[i - 4] = jnp.zeros((2, 24, 128), F32)
+            rb_early[i] = jnp.zeros((2, 16, 128), F32)
+            if i >= 4:
+                rb[i - 4] = jnp.zeros((24, 128), F32)
 
     loads[0].wait()
     spread = lax.broadcasted_iota(jnp.int32, (64, 512), 0) == (lax.broadcasted_iota(jnp.int32, (64, 512), 1) >> 3)
@@ -175,14 +174,14 @@
     def early(i):
         dx, dy = DIRS[i]
         return pltpu.make_async_remote_copy(
-            src_ref=t3_early, dst_ref=rb_early.at[i], send_sem=ssem2.at[i], recv_sem=rsem2.at[i],
+            src_ref=t3_early, dst_ref=rb_early.at[i], send_sem=ssem3.at[i], recv_sem=rsem3.at[i],
             device_id=(gx + dx, gy + dy), device_id_type=MESH,
         )
 
     def second(i):
         dx, dy = DIRS[i]
         return pltpu.make_async_remote_copy(
-            src_ref=t3, dst_ref=rb.at[i - 4], send_sem=ssem2.at[i], recv_sem=rsem2.at[i],
+            src_ref=t3, dst_ref=rb.at[i - 4], send_sem=ssem2.at[i - 4], recv_sem=rsem2.at[i - 4],
             device_id=(gx + dx, gy + dy), device_id_type=MESH,
         )
 
@@ -194,7 +193,7 @@
             def _():
                 getattr(make(i), action)()
 
-    corners, sides = range(4), range(4, 8)
+    sides = range(4, 8)
 
     on_all(first, "start", 1)
 
@@ -290,8 +289,12 @@
         rest = (src0[kr, 0:4, 0:16, :] - (r + 4.0) * own(early2, kr)) + beside_own(early2, kr)
         pair = fold(16, 4, kr, rest, pair)
     source1 = matmul(lhs[0:64, 0:512], down_table[0:512, :])
-    t3_early[0], t3_early[1], _ = down(cut(source1, 4), cut(reaction1, 4), None)
-    on_all(early, "start", 1, corners)
+    s3 = 0.25**3
+    source3, reaction3, _ = down(cut(source1, 4), cut(reaction1, 4), None)
+    w3 = DAMP / (reaction3 + 4.0 * s3)
+    t3_early[0] = w3 * source3
+    t3_early[1] = w3 * s3
+    on_all(early, "start", 1)
 
     on_all(first, "wait_recv", -1)
 
@@ -352,51 +355,29 @@
 
     source3, reaction3, levels = down(cut(source1, 4), cut(reaction1, 4), plane_in)
 
-    t3[0] = source3
-    t3[1] = reaction3
+    t3[...] = jnp.where(plane_in, DAMP / (reaction3 + 4.0 * s3), 0.0) * source3
     on_all(second, "start", 1, sides)
-    on_all(second, "wait_recv", -1, sides)
-    on_all(early, "wait_recv", -1, corners)
 
     lane8 = lanes_of((8, 128))
     sub8 = rows_of((8, 128))
-    own8 = (lane8 >= 29) & (lane8 < 99)
     high8 = lane8 >= 64
 
-    def arrived(dx, dy):
-        return rb.at[DIRS.index((-dx, -dy)) - 4]
-
-    def corner(a, dx, dy, start):
-        x = rb_early[DIRS.index((-dx, -dy)), a, start : start + 8, :]
-        if dx < 0 and start == 8:
-            return jnp.where(sub8 >= 6, arrived(0, dy)[a, 16:24, :], x)
-        if dx > 0 and start == 0:
-            return jnp.where(sub8 < 2, arrived(0, dy)[a, 16:24, :], x)
-        return x
-
-    def joined(a, dx, start):
-        if dx == 0:
-            middle = t3[a, start : start + 8, :]
-            left, right = (arrived(0, dy)[a, start : start + 8, :] for dy in (-1, 1))
-        else:
-            middle = arrived(dx, 0)[a, start : start + 8, :]
-            left, right = (corner(a, dx, dy, start) for dy in (-1, 1))
+    def joined(first_lane, middle, left, right):
+        own8 = (lane8 >= first_lane) & (lane8 < 128 - first_lane)
         return jnp.where(own8, middle, pltpu.roll(jnp.where(high8, left, right), 64, 1))
 
-    s3 = 0.25**3
-    for t in range(7):
-        if t == 4:
-            parts = [jnp.where(sub8 == 7, arrived(-1, 0)[a, 16:24, :], arrived(1, 0)[a, 16:24, :]) for a in range(2)]
-        else:
-            dx, start = ((0, 0), (0, 8), (1, 0), (1, 8), None, (-1, 0), (-1, 8))[t]
-            parts = [joined(a, dx, start) for a in range(2)]
-        spot = 8 * t + sub8
-        spot = jnp.where(spot >= 36, spot - 56, spot) + 16 * gx
-        side = lane8 - 32 + 64 * gy
-        inside = (spot >= 0) & (spot < 16 * gx_size) & (side >= 0) & (side < 64 * gy_size)
-        w = jnp.where(inside, DAMP / (parts[1] + 4.0 * s3), 0.0)
-        region[0, 8 * t : 8 * t + 8, :] = w * s3
-        region[1, 8 * t : 8 * t + 8, :] = w * parts[0]
+    def known(a, dx, dy, start):
+        x = t3_early if dx == 0 and dy == 0 else rb_early.at[DIRS.index((-dx, -dy))]
+        return x[a, start : start + 8, :]
+
+    region_rows = ((0, 0), (0, 8), (1, 0), (1, 8), None, (-1, 0), (-1, 8))
+
+    on_all(early, "wait_recv", -1)
+    region[0, 32:40, :] = jnp.zeros((8, 128), F32)
+    for t in (0, 1, 2, 3, 5, 6):
+        dx, start = region_rows[t]
+        region[0, 8 * t : 8 * t + 8, :] = joined(32, *(known(1, dx, dy, start) for dy in (0, -1, 1)))
+
     def tiles_around(x, width):
         if width == 0:
             return x
@@ -411,6 +392,31 @@
         return x[count : x.shape[0] - count]
 
     ws = turned(jnp.stack([region[0, pl.ds(t, 8, 7), :] for t in range(7)]), 2)
+    on_all(first, "wait_send", 1)
+    on_all(early, "wait_send", 1)
+    on_all(second, "wait_recv", -1, sides)
+
+    def arrived(dx, dy, start):
+        return rb[DIRS.index((-dx, -dy)) - 4, start : start + 8, :]
+
+    def corner(dx, dy, start):
+        x = known(0, dx, dy, start)
+        if dx < 0 and start == 8:
+            return jnp.where(sub8 >= 6, arrived(0, dy, 16), x)
+        if dx > 0 and start == 0:
+            return jnp.where(sub8 < 2, arrived(0, dy, 16), x)
+        return x
+
+    for t in range(7):
+        if t == 4:
+            part = jnp.where(sub8 == 7, arrived(-1, 0, 16), arrived(1, 0, 16))
+        else:
+            dx, start = region_rows[t]
+            if dx == 0:
+                part = joined(32, t3[start : start + 8, :], arrived(0, -1, start), arrived(0, 1, start))
+            else:
+                part = joined(29, arrived(dx, 0, start), corner(dx, -1, start), corner(dx, 1, start))
+        region[1, 8 * t : 8 * t + 8, :] = part
     wb = turned(jnp.stack([region[1, pl.ds(t, 8, 7), :] for t in range(7)]), 2)
     v = wb[0][2:9]
     for group in range((NC - 1) // 3):
@@ -441,13 +447,27 @@
     joint = jnp.concatenate([jnp.concatenate(row_planes, axis=1) for row_planes in correction], axis=0)
     fine = matmul(joint, up_table[...])
     for kr in range(8):
+        rows = 24 if kr in (0, 1, 6, 7) else 16
         k = kr // 2
-        c0 = jnp.stack([fine[24 * k : 24 * k + 24, c * 128 : (c + 1) * 128] for c in range(5)])
-        put(v2, kr, v2[kr + 1] + c0)
-    for kr in range(8):
-        x = v2[kr + 1]
-        src0[kr] = w0[kr] * src0[kr]
-        put(v1, kr, (0.2 * x + src0[kr]) + w0[kr] * beside0(v2, kr))
+        c0 = jnp.stack([fine[24 * k : 24 * k + rows, c * 128 : (c + 1) * 128] for c in range(5)])
+        x = v2[kr + 1, :, 0:rows, :] + c0
+        v2[kr + 1, :, 0:rows, :] = x
+        if kr == 7:
+            v2[0] = pltpu.roll(x, 1, 1)
+        if kr == 0:
+            v2[9] = pltpu.roll(x, 23, 1)
+    for kr in range(8):
+        rows = 24 if kr in (0, 7) else 16
+        near = (v2[kr, :, 0:rows, :] + v2[kr + 2, :, 0:rows, :]) + side_sum_0(v2[kr + 1, :, 0:rows, :], lane5[:, 0:rows, :])
+        w = w0[kr, :, 0:rows, :]
+        wb = w * src0[kr, :, 0:rows, :]
+        src0[kr, :, 0:rows, :] = wb
+        x = (0.2 * v2[kr + 1, :, 0:rows, :] + wb) + w * near
+        v1[kr + 1, :, 0:rows, :] = x
+        if kr == 7:
+            v1[0] = pltpu.roll(x, 1, 1)
+        if kr == 0:
+            v1[9] = pltpu.roll(x, 23, 1)
     for kr in range(8):
         x = v1[kr + 1]
         x = (0.2 * x + src0[kr]) + w0[kr] * beside0(v1, kr)
@@ -455,8 +475,6 @@
             out_vmem[c, pl.ds(kr, 16, 8), :] = x[c, 0:16]
     for c in range(4):
         out_ref[:, c * 128 : (c + 1) * 128] = out_vmem[c]
-    on_all(first, "wait_send", 1)
-    on_all(early, "wait_send", 1, corners)
     on_all(second, "wait_send", 1, sides)
 
 
@@ -484,13 +502,13 @@
                 pltpu.VMEM((512, 640), BF16),
                 pltpu.VMEM((2, 2, 64, 128), F32),
                 pltpu.VMEM((2, 2, 96, 128), F32),
-                pltpu.VMEM((2, 24, 128), F32),
-                pltpu.VMEM((4, 2, 24, 128), F32),
+                pltpu.VMEM((24, 128), F32),
+                pltpu.VMEM((4, 24, 128), F32),
                 pltpu.VMEM((2, 16, 128), F32),
-                pltpu.VMEM((4, 2, 16, 128), F32),
+                pltpu.VMEM((8, 2, 16, 128), F32),
                 pltpu.VMEM((2, 56, 128), F32),
                 pltpu.VMEM((4, 128, 128), F32),
-                dma((9,)), dma((8,)), dma((8,)), dma((8,)), dma((8,)),
+                dma((9,)), dma((8,)), dma((8,)), dma((4,)), dma((4,)), dma((8,)), dma((8,)),
             ],
             compiler_params=pltpu.CompilerParams(
                 collective_id=0, has_side_effects=True, vmem_limit_bytes=60 * 1024 * 1024

time: 18 us -> 17.8 us (0.989)
  Pallas kernels: 17.2 us -> 17 us
    pallas_call x1, Pallas kernels: 17.2 us -> 17 us  [per_device(): pl.pallas_call(functools.partial(kernel, gx_size, gy_size), out_shape=plt...]
where the time goes in v4:
time: 17.8 us; the launch traced here: 17.7 us
  Pallas kernels  17 us (96%)
  local copies, waits for them, and re-layouts  0.71 us (4%)
    pallas_call x1, Pallas kernels, per_device(): pl.pallas_call(functools.partial(kernel, gx_size, gy_size), out_shape=plt...  17 us
    unnamed x1, local copies, waits for them, and re-layouts  0.71 us

profile of v4, /device:TPU:38, one launch (start us, length us, event | category | flops | bytes accessed | tf_op | source)
XLA Modules:
  0.0 17.7 jit_solution(4204844079708351950)
XLA Ops:
  0.0 17.0 %v_cycle.1 = f32[128,512]{1,0:T(8,128)S(1)} custom-call(f32[128,512]{1,0:T(8,128)} %rs_hbm.1, f32[128,512]{1,0:T(8,128)} %kappa_hbm.1, s32[16,64]{1,0:T(8,128)} %ice_hbm.1), custom_call_target="tpu_custom_call" | custom-call | tf_op jit(solution)/shard_map/v_cycle/pallas_call | solution.py:486
  17.0 0.7 %copy.5 = f32[128,512]{1,0:T(8,128)} copy(f32[128,512]{1,0:T(8,128)S(1)} %v_cycle.1) | data formatting | bytes 524288

commit v5 on v4

--- a/solution.py
+++ b/solution.py
@@ -25,15 +25,11 @@
     return lax.broadcasted_iota(jnp.int32, shape, len(shape) - 2)
 
 
-def split(x):
+def matmul(x, table):
     high = x.astype(BF16)
     low = (x - high.astype(F32)).astype(BF16)
-    return high, low
-
-
-def matmul(x, table):
-    high, low = split(x)
-    return jnp.dot(high, table, preferred_element_type=F32) + jnp.dot(low, table, preferred_element_type=F32)
+    both = jnp.dot(jnp.concatenate([high, low], axis=0), table, preferred_element_type=F32)
+    return both[: x.shape[0]] + both[x.shape[0] :]
 
 
 def side_sum_0(x, lane):

time: 17.8 us -> 17.7 us (level)
  Pallas kernels: 17 us -> 16.8 us
where the time goes in v5:
time: 17.7 us; the launch traced here: 17.6 us
  Pallas kernels  16.8 us (95%)
  local copies, waits for them, and re-layouts  0.71 us (4%)
    pallas_call x1, Pallas kernels, per_device(): pl.pallas_call(functools.partial(kernel, gx_size, gy_size), out_shape=plt...  16.8 us
    unnamed x1, local copies, waits for them, and re-layouts  0.71 us

profile of v5, /device:TPU:38, one launch (start us, length us, event | category | flops | bytes accessed | tf_op | source)
XLA Modules:
  0.0 17.6 jit_solution(13314933143180940982)
XLA Ops:
  0.0 16.8 %v_cycle.1 = f32[128,512]{1,0:T(8,128)S(1)} custom-call(f32[128,512]{1,0:T(8,128)} %rs_hbm.1, f32[128,512]{1,0:T(8,128)} %kappa_hbm.1, s32[16,64]{1,0:T(8,128)} %ice_hbm.1), custom_call_target="tpu_custom_call" | custom-call | tf_op jit(solution)/shard_map/v_cycle/pallas_call | solution.py:482
  16.8 0.7 %copy.5 = f32[128,512]{1,0:T(8,128)} copy(f32[128,512]{1,0:T(8,128)S(1)} %v_cycle.1) | data formatting | bytes 524288

commit v6 on v5

--- a/solution.py
+++ b/solution.py
@@ -292,7 +292,25 @@
     t3_early[1] = w3 * s3
     on_all(early, "start", 1)
 
-    on_all(first, "wait_recv", -1)
+    row = rows_of((24, 128))
+    lane = lanes_of((24, 128))
+    row_in = ((row < 16) | ((row < 20) & (gx < gx_size - 1))) | ((row >= 20) & (gx > 0))
+    right_in = gy < gy_size - 1
+    left_in = gy > 0
+    tile_in = row_in & (((lane < 64) & right_in) | ((lane >= 64) & left_in))
+    plane_in = row_in & (((lane >= 32) & (lane < 96)) | ((lane >= 96) & right_in) | ((lane < 32) & left_in))
+    on_all(first, "wait_recv", -1, (6, 7))
+    halo_in = row_in[16:24, :]
+    for kr in range(8):
+        halo_r = jnp.stack([field[1, c, pl.ds(128 + kr, 8, 8), :] for c in range(4)])
+        halo_b = jnp.stack([field[0, c, pl.ds(128 + kr, 8, 8), :] for c in range(4)])
+        halo_w = jnp.where(halo_in, DAMP / (halo_r + 4.0), 0.0)
+        r0[kr, 0:4, 16:24, :] = halo_r
+        w0[kr, 0:4, 16:24, :] = halo_w
+        src0[kr, 0:4, 16:24, :] = halo_b
+        v1[kr + 1, 0:4, 16:24, :] = halo_w * halo_b
+
+    on_all(first, "wait_recv", -1, (4, 5, 0, 1, 2, 3))
 
     for a in range(2):
         for tt in range(12):
@@ -302,13 +320,6 @@
             field[a, 4, 16 * tt : 16 * tt + 8, :] = jnp.where(low8, from_right, turned)
             field[a, 4, 16 * tt + 8 : 16 * tt + 16, :] = jnp.where(low8, turned, from_left)
 
-    row = rows_of((24, 128))
-    lane = lanes_of((24, 128))
-    row_in = ((row < 16) | ((row < 20) & (gx < gx_size - 1))) | ((row >= 20) & (gx > 0))
-    right_in = gy < gy_size - 1
-    left_in = gy > 0
-    tile_in = row_in & (((lane < 64) & right_in) | ((lane >= 64) & left_in))
-    plane_in = row_in & (((lane >= 32) & (lane < 96)) | ((lane >= 96) & right_in) | ((lane < 32) & left_in))
     lane5 = lanes_of((5, 24, 128))
 
     def put(ref, kr, x):
@@ -321,23 +332,15 @@
     def beside0(ref, kr):
         return (ref[kr] + ref[kr + 2]) + side_sum_0(ref[kr + 1], lane5)
 
-    halo_in = row_in[16:24, :]
     pair = None
     for kr in range(8):
         tile_r = field[1, 4, pl.ds(kr, 24, 8), :]
         tile_b = field[0, 4, pl.ds(kr, 24, 8), :]
-        halo_r = jnp.stack([field[1, c, pl.ds(128 + kr, 8, 8), :] for c in range(4)])
-        halo_b = jnp.stack([field[0, c, pl.ds(128 + kr, 8, 8), :] for c in range(4)])
         tile_w = jnp.where(tile_in, DAMP / (tile_r + 4.0), 0.0)
-        halo_w = jnp.where(halo_in, DAMP / (halo_r + 4.0), 0.0)
         r0[kr, 4] = tile_r
-        r0[kr, 0:4, 16:24, :] = halo_r
         w0[kr, 4] = tile_w
-        w0[kr, 0:4, 16:24, :] = halo_w
         src0[kr, 4] = tile_b
-        src0[kr, 0:4, 16:24, :] = halo_b
         v1[kr + 1, 4] = tile_w * tile_b
-        v1[kr + 1, 0:4, 16:24, :] = halo_w * halo_b
         pair = fold(24, 5, kr, r0[kr], pair)
     v1[0] = pltpu.roll(v1[8], 1, 1)
     v1[9] = pltpu.roll(v1[1], 23, 1)

time: 17.7 us -> 17.7 us (level)
  no operation moved by 1% of the time
where the time goes in v6:
time: 17.7 us; the launch traced here: 17.5 us
  Pallas kernels  16.8 us (95%)
  local copies, waits for them, and re-layouts  0.71 us (4%)
    pallas_call x1, Pallas kernels, per_device(): pl.pallas_call(functools.partial(kernel, gx_size, gy_size), out_shape=plt...  16.8 us
    unnamed x1, local copies, waits for them, and re-layouts  0.71 us

profile of v6, /device:TPU:38, one launch (start us, length us, event | category | flops | bytes accessed | tf_op | source)
XLA Modules:
  0.0 17.5 jit_solution(2703945943974526099)
XLA Ops:
  0.0 16.8 %v_cycle.1 = f32[128,512]{1,0:T(8,128)S(1)} custom-call(f32[128,512]{1,0:T(8,128)} %rs_hbm.1, f32[128,512]{1,0:T(8,128)} %kappa_hbm.1, s32[16,64]{1,0:T(8,128)} %ice_hbm.1), custom_call_target="tpu_custom_call" | custom-call | tf_op jit(solution)/shard_map/v_cycle/pallas_call | solution.py:485
  16.8 0.7 %copy.5 = f32[128,512]{1,0:T(8,128)} copy(f32[128,512]{1,0:T(8,128)S(1)} %v_cycle.1) | data formatting | bytes 524288
